TPU v7x, 32 devices: a whole 2x2x4 slice. The times are simulated.
32 devices in a mesh: blk: 4 (over y, x), head: 4 (over z), grp: 2 (over core).
Axes of the slice: x: 2, y: 2, z: 4, core: 2. Of those that a mesh axis runs over, the one named last changes fastest.
Arguments:
- t_query: bfloat16 [4096, 4096], P('blk', ('head', 'grp')), may hold values from -80 to 80
- t_key: bfloat16 [4096, 4096], P('blk', ('head', 'grp')), may hold values from -80 to 80
- t_value: bfloat16 [4096, 4096], P('blk', ('head', 'grp')), may hold values from -6 to 6
- t_out: bfloat16 [4096, 4096], P(('head', 'grp')), may hold values from -0.09375 to 0.09375
- s_query: bfloat16 [4096, 2048], P('blk', ('head', 'grp')), may hold values from -80 to 80
- s_key: bfloat16 [4096, 2048], P('blk', ('head', 'grp')), may hold values from -80 to 80
- s_value: bfloat16 [4096, 2048], P('blk', ('head', 'grp')), may hold values from -6 to 6
- s_out: bfloat16 [2048, 4096], P(('head', 'grp')), may hold values from -0.125 to 0.125
- segments: int32 [4096], P('blk'), may hold values from 0 to 1, never falling along the last dimension, each value on 1 to 4032 neighbouring positions
- selection: int32 [64, 16], P('blk'), may hold values from 0 to 63, as said below
Outputs:
- mismatch: float32 [4096, 4096], P('blk', ('head', 'grp'))
- s_dq: float32 [4096, 2048], P('blk', ('head', 'grp'))
- s_dk: float32 [4096, 2048], P('blk', ('head', 'grp'))
- s_dv: float32 [4096, 2048], P('blk', ('head', 'grp'))
Inputs may be any that keep to these rules, and one draw needn't show every extreme that they name: `selection`: entry 0 of row b is b itself; for b >= 32, entry 1 of row b is b - 32; every entry of row b lies between 0 and b; entries of a row may repeat. `segments`: document numbers never fall along the sequence.
All inputs are finite; a program needn't handle non-finite values.
Results may differ from a plain program's by a relative error of at most 0.015.
Values may be sent and summed in bfloat16 or wider, within the bound.
A program may use at most 128 MiB of HBM per device.

v0:
```python
import math

import jax
import jax.numpy as jnp
from jax import lax
from jax.sharding import PartitionSpec as P

HD = 128
BS = 64
NSEL = 16


masked_score = -1e30


def shifted(block, axis, distance):
    devices = range(lax.axis_size(axis))
    route = [(i - distance, i) for i in devices if i - distance in devices]
    return lax.ppermute(block, axis, route)


def student_forward(queries, key_all, value_all, segment_all, selection, first_row):
    row_count = queries.shape[0]
    head_count = queries.shape[1] // HD
    blocks = row_count // BS
    query_blocks = queries.reshape(blocks, BS, head_count, HD)
    key_blocks = key_all.reshape(-1, BS, head_count, HD)[selection].reshape(
        blocks, NSEL * BS, head_count, HD
    )
    value_blocks = value_all.reshape(-1, BS, head_count, HD)[selection].reshape(
        blocks, NSEL * BS, head_count, HD
    )
    key_pos = (selection[:, :, None] * BS + jnp.arange(BS)[None, None, :]).reshape(
        blocks, NSEL * BS
    )
    query_pos = (first_row + jnp.arange(row_count)).reshape(blocks, BS)
    key_seg = segment_all[key_pos]
    query_seg = segment_all[query_pos]
    scores = jnp.einsum(
        "bqhd,bkhd->bhqk", query_blocks, key_blocks, preferred_element_type=jnp.float32
    ) * HD ** (-0.5)
    allowed = (
        (key_pos[:, None, :] <= query_pos[:, :, None])
        & (key_seg[:, None, :] == query_seg[:, :, None])
    )[:, None]
    scores = jnp.where(allowed, scores, masked_score)
    largest = jnp.max(scores, axis=3, keepdims=True)
    weights = jnp.where(allowed, jnp.exp(scores - largest), 0.0)
    weights = weights / jnp.sum(weights, axis=3, keepdims=True)
    value_wide = value_blocks.astype(jnp.float32)
    blended = jnp.einsum("bhqk,bkhd->bqhd", weights, value_wide, precision=lax.Precision.HIGHEST)
    saved = (query_blocks, key_blocks, value_wide, weights, blended)
    return (blended.reshape(row_count, head_count * HD), saved)


def student_backward(grad_attn, saved, selection, token_count):
    query_blocks, key_blocks, value_wide, weights, blended = saved
    blocks, _, head_count, _ = query_blocks.shape
    row_count = blocks * BS
    grad_blocks = grad_attn.reshape(blocks, BS, head_count, HD)
    value_grad = jnp.einsum(
        "bhqk,bqhd->bkhd", weights, grad_blocks, precision=lax.Precision.HIGHEST
    )
    weight_grad = jnp.einsum(
        "bqhd,bkhd->bhqk", grad_blocks, value_wide, precision=lax.Precision.HIGHEST
    )
    row_dots = jnp.sum(grad_blocks * blended, axis=3).transpose(0, 2, 1)[..., None]
    score_grad = weights * (weight_grad - row_dots) * HD ** (-0.5)
    query_grad = jnp.einsum(
        "bhqk,bkhd->bqhd",
        score_grad,
        key_blocks.astype(jnp.float32),
        precision=lax.Precision.HIGHEST,
    )
    key_grad = jnp.einsum(
        "bhqk,bqhd->bkhd",
        score_grad,
        query_blocks.astype(jnp.float32),
        precision=lax.Precision.HIGHEST,
    )
    flat_sel = selection.reshape(-1)
    width = head_count * HD
    key_total = (
        jnp.zeros((token_count // BS, BS, width), jnp.float32)
        .at[flat_sel]
        .add(key_grad.reshape(blocks * NSEL, BS, width))
    )
    value_total = (
        jnp.zeros((token_count // BS, BS, width), jnp.float32)
        .at[flat_sel]
        .add(value_grad.reshape(blocks * NSEL, BS, width))
    )
    return (
        query_grad.reshape(row_count, width),
        key_total.reshape(token_count, width),
        value_total.reshape(token_count, width),
    )


def teacher_update(
    carried, key_rows, value_rows, seg_rows, first_key, queries, query_seg, query_pos
):
    running_max, running_sum, weighted = carried
    head_count = queries.shape[1]
    key_heads = key_rows.reshape(key_rows.shape[0], head_count, HD)
    value_heads = value_rows.reshape(value_rows.shape[0], head_count, HD)
    scores = jnp.einsum(
        "qhd,khd->hqk", queries, key_heads, preferred_element_type=jnp.float32
    ) * HD ** (-0.5)
    key_pos = first_key + jnp.arange(key_rows.shape[0])
    allowed = (
        (key_pos[None, :] <= query_pos[:, None]) & (seg_rows[None, :] == query_seg[:, None])
    )[None]
    scores = jnp.where(allowed, scores, masked_score)
    new_max = jnp.maximum(running_max, jnp.max(scores, axis=2))
    factor = jnp.exp(running_max - new_max)
    weights = jnp.where(allowed, jnp.exp(scores - new_max[..., None]), 0.0)
    running_sum = factor * running_sum + jnp.sum(weights, axis=2)
    product = jnp.einsum(
        "hqk,khd->hqd",
        weights.astype(jnp.bfloat16),
        value_heads,
        preferred_element_type=jnp.float32,
    )
    weighted = factor[..., None] * weighted + product
    return (new_max, running_sum, weighted)


def teacher_fold(carried, key_rows, value_rows, seg_rows, queries, query_seg, query_pos):
    piece_rows = key_rows.shape[0]
    block_rows = math.gcd(piece_rows, 512)
    turn_count = piece_rows // block_rows
    last_query = query_pos[-1]

    def one_turn(turn_index, status):
        offset = turn_index * block_rows
        key_block = lax.dynamic_slice_in_dim(key_rows, offset, block_rows, 0)
        value_block = lax.dynamic_slice_in_dim(value_rows, offset, block_rows, 0)
        seg_block = lax.dynamic_slice_in_dim(seg_rows, offset, block_rows, 0)

        def compute(inner):
            return teacher_update(
                inner, key_block, value_block, seg_block, offset, queries, query_seg, query_pos
            )

        def keep(inner):
            return inner

        return lax.cond(offset > last_query, keep, compute, status)

    return lax.fori_loop(0, turn_count, one_turn, carried)


def on_device(t_query, t_key, t_value, t_out, s_query, s_key, s_value, s_out, segments, selection):
    row_count = t_query.shape[0]
    head_count = t_query.shape[1] // HD
    cycle_size = lax.axis_size("blk")
    my_index = lax.axis_index("blk")
    first_row = my_index * row_count
    token_count = row_count * cycle_size
    query_pos = first_row + jnp.arange(row_count)
    queries = t_query.reshape(row_count, head_count, HD)
    initial = (
        jnp.full((head_count, row_count), masked_score, jnp.float32),
        jnp.zeros((head_count, row_count), jnp.float32),
        jnp.zeros((head_count, row_count, HD), jnp.float32),
    )
    teacher_state = teacher_fold(
        initial,
        lax.all_gather(t_key, "blk", axis=0, tiled=True),
        lax.all_gather(t_value, "blk", axis=0, tiled=True),
        lax.all_gather(segments, "blk", axis=0, tiled=True),
        queries,
        segments,
        query_pos,
    )
    key_full, value_full, seg_full = (
        lax.all_gather(s_key, "blk", axis=0, tiled=True),
        lax.all_gather(s_value, "blk", axis=0, tiled=True),
        lax.all_gather(segments, "blk", axis=0, tiled=True),
    )
    t_attn = (
        (teacher_state[2] / teacher_state[1][..., None])
        .transpose(1, 0, 2)
        .reshape(row_count, head_count * HD)
    )
    t_attn = t_attn.astype(jnp.bfloat16)
    student_full, saved = student_forward(
        s_query, key_full, value_full, seg_full, selection, first_row
    )
    s_attn = student_full.astype(jnp.bfloat16)
    partial_terms = jnp.dot(s_attn, s_out, preferred_element_type=jnp.float32) - jnp.dot(
        t_attn, t_out, preferred_element_type=jnp.float32
    )
    contract = (((1,), (1,)), ((), ()))
    mismatch = lax.psum_scatter(
        partial_terms.astype(jnp.bfloat16), ("head", "grp"), scatter_dimension=1, tiled=True
    ).astype(jnp.float32)
    grad_attn = lax.dot_general(
        lax.all_gather(mismatch.astype(jnp.bfloat16), ("head", "grp"), axis=1, tiled=True),
        s_out,
        contract,
        preferred_element_type=jnp.float32,
    )
    grad_query, grad_keys, grad_values = student_backward(grad_attn, saved, selection, token_count)
    key_grads = lax.dynamic_slice_in_dim(grad_keys, first_row, row_count, 0)
    value_grads = lax.dynamic_slice_in_dim(grad_values, first_row, row_count, 0)
    for distance in range(1, cycle_size):
        owner = my_index - distance
        owner_start = jnp.maximum(owner, 0) * row_count
        live = owner >= 0
        key_slab = jnp.where(
            live, lax.dynamic_slice_in_dim(grad_keys, owner_start, row_count, 0), 0.0
        )
        value_slab = jnp.where(
            live, lax.dynamic_slice_in_dim(grad_values, owner_start, row_count, 0), 0.0
        )
        key_in, value_in = (
            shifted(key_slab.astype(jnp.bfloat16), "blk", -distance).astype(key_slab.dtype),
            shifted(value_slab.astype(jnp.bfloat16), "blk", -distance).astype(value_slab.dtype),
        )
        key_grads = key_grads + key_in
        value_grads = value_grads + value_in
    return (mismatch, grad_query, key_grads, value_grads)


def solution(mesh):
    in_specs = (
        P("blk", ("head", "grp")),
        P("blk", ("head", "grp")),
        P("blk", ("head", "grp")),
        P(("head", "grp"), None),
        P("blk", ("head", "grp")),
        P("blk", ("head", "grp")),
        P("blk", ("head", "grp")),
        P(("head", "grp"), None),
        P("blk"),
        P("blk", None),
    )
    out_specs = (
        P("blk", ("head", "grp")),
        P("blk", ("head", "grp")),
        P("blk", ("head", "grp")),
        P("blk", ("head", "grp")),
    )
    return jax.shard_map(
        on_device, mesh=mesh, in_specs=in_specs, out_specs=out_specs, check_vma=False
    )
```

profile of v0, /device:TPU:0, one launch (start us, length us, event | category | flops | bytes accessed | tf_op | source)
XLA Modules:
  0.0 807.6 jit_solution(1042524988778419716)
XLA Ops:
  8.7 2.3 copy.97
  11.1 2.3 copy.99
  18.1 2.0 reshape.261
  20.2 9.9 %all_gather.20 = s32[4096]{0:T(1024)S(1)} all-gather(s32[1024]{0:T(1024)S(1)} %copy-done.12), channel_id=1, replica_groups=mesh['blk'=4,'head'=4,'grp'=2] {'blk'}, dimensions={0}, use_global_device_ids=true | all-gather | bytes 20480 | tf_op jit(solution)/shard_map/all_gather | solution.py:180
  30.1 6.1 gather_fusion.2
  36.4 90.5 %gather_fusion.1 = s32[16384]{0:T(1024)S(1)} fusion(s32[4096]{0:T(1024)S(1)} %all_gather.20, s32[16384]{0:T(1024)S(1)} %broadcast_clamp_fusion), kind=kCustom, calls=%fused_computation.1 | custom fusion | bytes 196608 | tf_op jit(solution)/shard_map/gather | solution.py:37
  129.0 4.0 reshape.259
  133.0 3.5 copy.91
  136.4 10.3 %gather_fusion.3 = bf16[256,64,2,128]{3,1,2,0:T(8,128)(2,1)} fusion(bf16[64,64,2,128]{3,1,2,0:T(8,128)(2,1)} %copy.91, s32[1024]{0:T(1024)S(1)} %pad_clamp_fusion), kind=kCustom, calls=%fused_computation.3 | custom fusion | bytes 16778240 | tf_op jit(solution)/shard_map/gather | solution.py:27
  146.7 9.7 %copy.92 = bf16[256,64,2,128]{3,1,0,2:T(8,128)(2,1)} copy(bf16[256,64,2,128]{3,1,2,0:T(8,128)(2,1)} %gather_fusion.3) | data formatting | bytes 16777216 | tf_op jit(solution)/shard_map/gather | solution.py:27
  156.4 4.0 reshape.257
  160.4 3.5 copy.89
  163.9 10.4 %gather_fusion = bf16[256,64,2,128]{3,1,2,0:T(8,128)(2,1)} fusion(bf16[64,64,2,128]{3,1,2,0:T(8,128)(2,1)} %copy.89, s32[1024]{0:T(1024)S(1)} %pad_clamp_fusion), kind=kCustom, calls=%fused_computation | custom fusion | bytes 16778240 | tf_op jit(solution)/shard_map/gather | solution.py:30
  174.3 9.2 %copy.90 = bf16[256,64,2,128]{3,1,0,2:T(8,128)(2,1)} copy(bf16[256,64,2,128]{3,1,2,0:T(8,128)(2,1)} %gather_fusion) | data formatting | bytes 16777216 | tf_op jit(solution)/shard_map/gather | solution.py:30
  183.5 9.7 %fusion.20 = f32[16,2,1024,64]{2,3,1,0:T(8,128)} fusion(bf16[16,1024,2,128]{3,1,0,2:T(8,128)(2,1)} %bitcast.75, bf16[16,64,2,128]{3,2,1,0:T(2,128)(2,1)S(1)} %copy-done.4), kind=kOutput, calls=%fused_computation.38 | convolution fusion | flops 536870912 | bytes 17301504 | tf_op jit(solution)/shard_map/bqhd,bkhd->bhqk/dot_general | solution.py:39
  193.3 13.0 %fusion.43 = (f32[16,2,64]{2,1,0:T(2,128)S(1)}, f32[16,2,64,1024]{3,2,1,0:T(8,128)}) fusion(f32[16,2,1024,64]{2,3,1,0:T(8,128)} %fusion.20, pred[16,64,1024]{2,1,0:T(8,128)(4,1)S(1)} %copy-done.7), kind=kOutput, calls=%fused_computation.79 | output fusion | flops 14681087 | bytes 17833984 | tf_op jit(solution)/shard_map/sub | solution.py:48
  206.3 9.2 %fusion.44 = (bf16[16,64,2,128]{3,1,2,0:T(8,128)(2,1)S(1)}, f32[16,64,2,128]{3,1,2,0:T(8,128)}) fusion(f32[16,2,64,1024]{3,2,1,0:T(8,128)} %get-tuple-element.437, f32[16,2,64]{2,1,0:T(2,128)S(1)} %get-tuple-element.436, bf16[16,1024,2,128]{3,1,0,2:T(8,128)(2,1)} %bitcast.79), kind=kOutput, calls=%fused_computation.80 | convolution fusion | flops 3223584768 | bytes 18358272 | tf_op jit(solution)/shard_map/bhqk,bkhd->bqhd/dot_general | solution.py:51
  218.3 28.4 %while.18 = (s32[]{:T(128)}, f32[4,1024]{1,0:T(4,128)S(1)}, f32[4,1024]{1,0:T(4,128)S(1)}, f32[4,1024,128]{2,1,0:T(8,128)}, s32[]{:T(128)}, /*index=5*/s32[4096]...) while((s32[]{:T(128)}, f32[4,1024]{1,0:T(4,128)S(1)}, ...), condition=%wide.region_7.8_spmd.clone, body=%wide.region_2.7_spmd.clone.sunk | while | flops 1103635968 | bytes 52722064 | solution.py:151
  219.4 11.0 %conditional.3 = (f32[4,1024]{1,0:T(4,128)S(1)}, f32[4,1024]{1,0:T(4,128)S(1)}, f32[4,1024,128]{2,1,0:T(8,128)}) conditional(s32[]{:T(128)} %convert_element_type.114, (s32[]{:T(128)}, s32[]{:T(128)}, s32[4096]{0:T(1024)S(1)}, s32[1024]{0:T(1024)S(1)}, bf16[4096,512]{0,1:T(8,128)(2,1)}, /*index=5*/bf16[1024,4,128]{2,0,1:T(8,128)(2,1)S(1)}, ...), branch_computations={%region_3.5_spmd, %region_6.6_spmd} | conditional | flops 1103635968 | bytes 52684932 | solution.py:149
  223.1 2.1 fusion.4
  225.3 3.8 multiply_add_fusion
  231.1 11.0 %conditional.3 = (f32[4,1024]{1,0:T(4,128)S(1)}, f32[4,1024]{1,0:T(4,128)S(1)}, f32[4,1024,128]{2,1,0:T(8,128)}) conditional(s32[]{:T(128)} %convert_element_type.114, (s32[]{:T(128)}, s32[]{:T(128)}, s32[4096]{0:T(1024)S(1)}, s32[1024]{0:T(1024)S(1)}, bf16[4096,512]{0,1:T(8,128)(2,1)}, /*index=5*/bf16[1024,4,128]{2,0,1:T(8,128)(2,1)S(1)}, ...), branch_computations={%region_3.5_spmd, %region_6.6_spmd} | conditional | flops 1103635968 | bytes 52684932 | solution.py:149
  234.8 2.1 fusion.4
  237.0 3.8 multiply_add_fusion
  246.7 3.0 copy.101
  251.5 10.4 %fusion.45 = f32[1024,4096]{1,0:T(8,128)} fusion(bf16[1024,512]{0,1:T(8,128)(2,1)S(1)} %bitcast.83, bf16[512,4096]{1,0:T(8,128)(2,1)} %param.17), kind=kOutput, calls=%fused_computation.81 | convolution fusion | flops 4294967296 | bytes 22020096 | tf_op jit(solution)/shard_map/dot_general | solution.py:192
  261.9 11.4 %subtract_convert_fusion = bf16[1024,4096]{1,0:T(8,128)(2,1)} fusion(f32[1024,4096]{1,0:T(8,128)} %fusion.45, bf16[256,4096]{1,0:T(8,128)(2,1)S(1)} %copy-done, bf16[128,8,2,128]{3,2,1,0:T(2,128)(2,1)S(1)} %bitcast.84), kind=kOutput, calls=%fused_computation.26 | convolution fusion | flops 2155872256 | bytes 27787264 | tf_op jit(solution)/shard_map/dot_general | solution.py:192
  273.4 155.0 %reduce-scatter.2.cloned.1.call-done = bf16[1024,512]{1,0:T(8,128)(2,1)} async-done(((bf16[1024,4096]{1,0:T(8,128)(2,1)}), bf16[1024,512]{1,0:T(8,128)(2,1)}) %reduce-scatter.2.cloned.1.call-update) | async-done | bytes 1048592 | tf_op jit(solution)/shard_map/reduce_scatter | solution.py:196
  428.5 2.8 convert_element_type.80
  431.3 79.0 %all-gather.14.cloned.1.call-done = bf16[1024,4096]{1,0:T(8,128)(2,1)} async-done(((bf16[1024,512]{1,0:T(8,128)(2,1)}), bf16[1024,4096]{1,0:T(8,128)(2,1)}) %all-gather.14.cloned.1.call-update) | async-done | bytes 8388624 | tf_op jit(solution)/shard_map/all_gather | solution.py:200
  510.3 6.7 fusion.46
  519.2 14.6 %multiply_multiply_fusion = f32[16,2,64,1024]{3,2,1,0:T(8,128)} fusion(f32[16,2,64]{2,1,0:T(2,128)S(1)} %bitcast.87, bf16[16,1024,2,128]{3,1,0,2:T(8,128)(2,1)} %bitcast.80, f32[16,64,2,128]{3,2,1,0:T(2,128)S(1)} %reshape.263, f32[16,2,64,1024]{3,2,1,0:T(8,128)} %get-tuple-element.437, f32[16,2,64]{2,1,0:T(2,128)S(1)} %get-tuple-element.436), kind=kOutput, calls=%fused_computation.30 | convolution fusion | flops 3229614080 | bytes 26230784 | tf_op jit(solution)/shard_map/bqhd,bkhd->bhqk/dot_general | solution.py:64
  533.8 15.8 %convolution_bitcast_fusion.1 = f32[16,1024,2,128]{3,1,2,0:T(8,128)S(1)} fusion(f32[16,2,64,1024]{3,2,1,0:T(8,128)} %multiply_multiply_fusion, bf16[16,64,2,128]{3,2,1,0:T(2,128)(2,1)S(1)} %copy-done.5), kind=kOutput, calls=%fused_computation.28 | convolution fusion | flops 3221225472 | bytes 25690112 | tf_op jit(solution)/shard_map/bhqk,bqhd->bkhd/dot_general | solution.py:75
  549.6 14.4 %copy.108 = f32[16,1024,2,128]{3,2,1,0:T(2,128)} copy(f32[16,1024,2,128]{3,1,2,0:T(8,128)S(1)} %convolution_bitcast_fusion.1) | data formatting | bytes 33554432 | tf_op jit(solution)/shard_map/bhqk,bqhd->bkhd/transpose | solution.py:75
  564.1 21.8 %reshape.306 = f32[256,64,256]{2,1,0:T(8,128)} reshape(f32[16,1024,2,128]{3,2,1,0:T(2,128)} %copy.108) | data formatting | bytes 33554432 | tf_op jit(solution)/shard_map/reshape | solution.py:86
  585.8 2.5 broadcast.206.clone
  588.3 52.1 %scatter_fusion = f32[64,64,256]{2,1,0:T(8,128)} fusion(f32[64,64,256]{2,1,0:T(8,128)} %broadcast.206.clone, s32[256]{0:T(256)S(1)} %bitcast.88, f32[256,64,256]{2,1,0:T(8,128)} %reshape.306), kind=kCustom, calls=%fused_computation.4 | custom fusion | flops 4194304 | bytes 50332672 | tf_op jit(solution)/shard_map/scatter-add | solution.py:86
  640.4 2.3 select_convert_fusion.5
  644.0 19.1 %convolution_bitcast_fusion = f32[16,1024,2,128]{1,3,2,0:T(8,128)} fusion(f32[16,64,2,128]{3,2,1,0:T(2,128)S(1)} %reshape.263, f32[16,2,64,1024]{3,2,1,0:T(8,128)} %get-tuple-element.437, f32[16,2,64]{2,1,0:T(2,128)S(1)} %get-tuple-element.436), kind=kOutput, calls=%fused_computation.27 | convolution fusion | flops 3223322624 | bytes 26222592 | tf_op jit(solution)/shard_map/bhqk,bqhd->bkhd/dot_general | solution.py:61
  665.7 25.0 %copy.110 = f32[16,1024,2,128]{3,2,1,0:T(2,128)} copy(f32[16,1024,2,128]{1,3,2,0:T(8,128)} %convolution_bitcast_fusion) | data formatting | bytes 33554432 | tf_op jit(solution)/shard_map/bhqk,bqhd->bkhd/transpose | solution.py:61
  690.8 21.6 %reshape.314 = f32[256,64,256]{2,1,0:T(8,128)} reshape(f32[16,1024,2,128]{3,2,1,0:T(2,128)} %copy.110) | data formatting | bytes 33554432 | tf_op jit(solution)/shard_map/reshape | solution.py:91
  712.3 2.4 broadcast.206.clone.1
  714.8 52.3 %scatter_fusion.1 = f32[64,64,256]{2,1,0:T(8,128)} fusion(f32[64,64,256]{2,1,0:T(8,128)} %broadcast.206.clone.1, s32[256]{0:T(256)S(1)} %bitcast.89, f32[256,64,256]{2,1,0:T(8,128)} %reshape.314), kind=kCustom, calls=%fused_computation.5 | custom fusion | flops 4194304 | bytes 50332672 | tf_op jit(solution)/shard_map/scatter-add | solution.py:91
  767.1 2.4 select_convert_fusion.2
  774.2 8.4 %fusion.28 = f32[16,64,2,128]{3,1,2,0:T(8,128)S(1)} fusion(f32[16,2,64,1024]{3,2,1,0:T(8,128)} %multiply_multiply_fusion, bf16[16,1024,2,128]{3,1,0,2:T(8,128)(2,1)} %bitcast.76), kind=kOutput, calls=%fused_computation.47 | convolution fusion | flops 3221225472 | bytes 17825792 | tf_op jit(solution)/shard_map/bhqk,bkhd->bqhd/dot_general | solution.py:69
  784.4 2.7 convert_add_fusion.1
  788.9 9.0 %collective-permute-done.4 = bf16[1024,256]{1,0:T(8,128)(2,1)S(1)} collective-permute-done((bf16[1024,256]{1,0:T(8,128)(2,1)S(1)}, bf16[1024,256]{1,0:T(8,128)(2,1)S(1)}, u32[]{:S(2)}, u32[]{:S(2)}) %collective-permute-start.4) | collective-permute-done | bytes 524320 | tf_op jit(solution)/shard_map/ppermute | solution.py:19
  797.9 2.4 convert_add_fusion
  (137 shorter events, 37.9 us)
Async XLA Ops:
  7.2 254.7 %copy-start = (bf16[256,4096]{1,0:T(8,128)(2,1)S(1)}, bf16[256,4096]{1,0:T(8,128)(2,1)}, u32[]{:S(2)}) copy-start(bf16[256,4096]{1,0:T(8,128)(2,1)} %param.21) | copy-start | bytes 6291460
  7.2 7.9 copy-start.8
  7.2 13.0 %copy-start.12 = (s32[1024]{0:T(1024)S(1)}, s32[1024]{0:T(1024)}, u32[]{:S(2)}) copy-start(s32[1024]{0:T(1024)} %param.22) | copy-start | bytes 12292
  7.2 121.8 %all-gather.8.cloned.1.call-start = ((), (), s32[]{:S(2)}) async-start(), calls=%async_computation.2 | async-start | bytes 2621440 | tf_op jit(solution)/shard_map/all_gather | solution.py:178
  7.9 148.5 %all-gather.6.cloned.1.call-start = ((), (), s32[]{:S(2)}) async-start(), calls=%async_computation.1 | async-start | bytes 2621440 | tf_op jit(solution)/shard_map/all_gather | solution.py:179
  8.7 208.2 %all-gather.10.cloned.1.call-start = ((), (), s32[]{:S(2)}) async-start(), calls=%async_computation.3 | async-start | bytes 5242880 | tf_op jit(solution)/shard_map/all_gather | solution.py:170
  11.0 205.8 %all-gather.12.cloned.1.call-start = ((), (), s32[]{:S(2)}) async-start(), calls=%async_computation.4 | async-start | bytes 5242880 | tf_op jit(solution)/shard_map/all_gather | solution.py:171
  13.4 415.0 %reduce-scatter.2.cloned.1.call-start = ((), (), s32[]{:S(2)}) async-start(), calls=%async_computation.5 | async-start | bytes 9437184 | tf_op jit(solution)/shard_map/reduce_scatter | solution.py:196
  174.3 9.3 %copy-start.4 = (bf16[16,64,2,128]{3,2,1,0:T(2,128)(2,1)S(1)}, bf16[16,64,2,128]{3,2,1,0:T(2,128)(2,1)}, u32[]{:S(2)}) copy-start(bf16[16,64,2,128]{3,2,1,0:T(2,128)(2,1)} %reshape.261) | copy-start | bytes 1572868
  183.5 9.7 %copy-start.7 = (pred[16,64,1024]{2,1,0:T(8,128)(4,1)S(1)}, pred[16,64,1024]{2,1,0:T(8,128)(4,1)}, u32[]{:S(2)}) copy-start(pred[16,64,1024]{2,1,0:T(8,128)(4,1)} %compare_and_fusion.1) | copy-start | bytes 3145732
  221.3 4.0 copy-start.2
  229.1 1.3 copy-start.3
  233.0 4.0 copy-start.2
  240.7 1.3 copy-start.3
  251.5 10.4 %copy-start.6 = (bf16[16,64,2,128]{3,2,1,0:T(2,128)(2,1)S(1)}, bf16[16,64,2,128]{3,2,1,0:T(2,128)(2,1)}, u32[]{:S(2)}) copy-start(bf16[16,64,2,128]{3,2,1,0:T(2,128)(2,1)} %copy.96) | copy-start | bytes 1572868
  273.3 155.1 %copy-start.13 = (s32[16,16]{1,0:T(8,128)S(1)}, s32[16,16]{1,0:T(8,128)}, u32[]{:S(2)}) copy-start(s32[16,16]{1,0:T(8,128)} %param.23) | copy-start | bytes 3076
  273.3 237.0 %all-gather.14.cloned.1.call-start = ((), (), s32[]{:S(2)}) async-start(), calls=%async_computation.6 | async-start | bytes 9437184 | tf_op jit(solution)/shard_map/all_gather | solution.py:200
  431.3 87.5 %copy-start.9 = (f32[16,64,2,128]{3,1,2,0:T(8,128)S(1)}, f32[16,64,2,128]{3,1,2,0:T(8,128)}, u32[]{:S(2)}) copy-start(f32[16,64,2,128]{3,1,2,0:T(8,128)} %get-tuple-element.439) | copy-start | bytes 3145732
  519.2 14.6 %copy-start.5 = (bf16[16,64,2,128]{3,2,1,0:T(2,128)(2,1)S(1)}, bf16[16,64,2,128]{3,2,1,0:T(2,128)(2,1)}, u32[]{:S(2)}) copy-start(bf16[16,64,2,128]{3,2,1,0:T(2,128)(2,1)} %reshape.261) | copy-start | bytes 1572868
  642.7 129.3 %collective-permute-start.2 = (bf16[1024,256]{1,0:T(8,128)(2,1)S(1)}, bf16[1024,256]{1,0:T(8,128)(2,1)S(1)}, u32[]{:S(2)}, u32[]{:S(2)}) collective-permute-start(bf16[1024,256]{1,0:T(8,128)(2,1)S(1)} %get-tuple-element.432), channel_id=1, source_target_pairs={{24,0},{25,1},{26,2},{27,3},{28,4},{29,5},{30,6},{31,7}} | collective-permute-start | bytes 1572872 | tf_op jit(solution)/shard_map/ppermute | solution.py:19
  663.2 121.3 %collective-permute-start.1 = (bf16[1024,256]{1,0:T(8,128)(2,1)S(1)}, bf16[1024,256]{1,0:T(8,128)(2,1)}, u32[]{:S(2)}, u32[]{:S(2)}) collective-permute-start(bf16[1024,256]{1,0:T(8,128)(2,1)S(1)} %get-tuple-element.433), channel_id=1, source_target_pairs={{16,0},{24,8},{17,1},{25,9},{18,2},{26,10},{19,3},{27,11},{20,4},{... | collective-permute-start | bytes 1572872 | tf_op jit(solution)/shard_map/ppermute | solution.py:19
  664.4 120.0 %collective-permute-start = (bf16[1024,256]{1,0:T(8,128)(2,1)S(1)}, bf16[1024,256]{1,0:T(8,128)(2,1)}, u32[]{:S(2)}, u32[]{:S(2)}) collective-permute-start(bf16[1024,256]{1,0:T(8,128)(2,1)S(1)} %get-tuple-element.431), channel_id=1, source_target_pairs={{8,0},{16,8},{24,16},{9,1},{17,9},{25,17},{10,2},{18,10},{26,18},{... | collective-permute-start | bytes 1572872 | tf_op jit(solution)/shard_map/ppermute | solution.py:19
  769.4 19.5 %collective-permute-start.5 = (bf16[1024,256]{1,0:T(8,128)(2,1)S(1)}, bf16[1024,256]{1,0:T(8,128)(2,1)S(1)}, u32[]{:S(2)}, u32[]{:S(2)}) collective-permute-start(bf16[1024,256]{1,0:T(8,128)(2,1)S(1)} %get-tuple-element.429), channel_id=1, source_target_pairs={{24,0},{25,1},{26,2},{27,3},{28,4},{29,5},{30,6},{31,7}} | collective-permute-start | bytes 1572872 | tf_op jit(solution)/shard_map/ppermute | solution.py:19
  770.7 27.2 %collective-permute-start.4 = (bf16[1024,256]{1,0:T(8,128)(2,1)S(1)}, bf16[1024,256]{1,0:T(8,128)(2,1)S(1)}, u32[]{:S(2)}, u32[]{:S(2)}) collective-permute-start(bf16[1024,256]{1,0:T(8,128)(2,1)S(1)} %get-tuple-element.430), channel_id=1, source_target_pairs={{16,0},{24,8},{17,1},{25,9},{18,2},{26,10},{19,3},{27,11},{20,4},{... | collective-permute-start | bytes 1572872 | tf_op jit(solution)/shard_map/ppermute | solution.py:19
  772.0 0.8 copy-start.10
  772.8 25.1 %collective-permute-start.3 = (bf16[1024,256]{1,0:T(8,128)(2,1)S(1)}, bf16[1024,256]{1,0:T(8,128)(2,1)S(1)}, u32[]{:S(2)}, u32[]{:S(2)}) collective-permute-start(bf16[1024,256]{1,0:T(8,128)(2,1)S(1)} %get-tuple-element.428), channel_id=1, source_target_pairs={{8,0},{16,8},{24,16},{9,1},{17,9},{25,17},{10,2},{18,10},{26,18},{... | collective-permute-start | bytes 1572872 | tf_op jit(solution)/shard_map/ppermute | solution.py:19
  774.1 10.3 %copy-start.11 = (bf16[1024,256]{1,0:T(8,128)(2,1)S(1)}, bf16[1024,256]{1,0:T(8,128)(2,1)}, u32[]{:S(2)}) copy-start(bf16[1024,256]{1,0:T(8,128)(2,1)} %copy-done.10) | copy-start | bytes 1572868
  774.1 26.2 %copy-start.1 = (bf16[256,4096]{1,0:T(8,128)(2,1)S(1)}, bf16[256,4096]{1,0:T(8,128)(2,1)}, u32[]{:S(2)}) copy-start(bf16[256,4096]{1,0:T(8,128)(2,1)} %param.21) | copy-start | bytes 6291460
Sparse Core Ops, SparseCore 0:
  9.9 37.9 all-gather.7
  49.7 35.1 all-gather.5
  87.4 52.5 all-gather.9
  142.2 52.5 all-gather.11
  273.4 154.8 reduce-scatter.1
  429.8 80.4 all-gather.13
where the time goes:
time: 820 us; the launch traced here: 808 us
  local copies, waits for them, and re-layouts  265 us (32%)
  waiting for transfers between devices  246 us (30%)
  other arithmetic  140 us (17%)
  matrix products  117 us (14%)
  between operations  14.9 us (2%)
  blocking collectives  9.88 us (1%)
    reduce_scatter x1, waiting for transfers between devices, on_device(): lax.psum_scatter(partial_terms.astype(jnp.bfloat16), ('head', 'grp'), sca...  155 us
    gather x2, local copies, waits for them, and re-layouts, student_forward(): key_seg = segment_all[key_pos]  90.6 us
    all_gather x1, waiting for transfers between devices, on_device(): lax.all_gather(mismatch.astype(jnp.bfloat16), ('head', 'grp'), axis=1, ti...  79 us
    scatter-add x1, other arithmetic, student_backward(): value_total = jnp.zeros((token_count // BS, BS, width), jnp.float32).at[f...  52.3 us
    scatter-add x1, other arithmetic, student_backward(): key_total = jnp.zeros((token_count // BS, BS, width), jnp.float32).at[fla...  52.1 us
    transpose x1, local copies, waits for them, and re-layouts, student_backward(): jnp.einsum('bhqk,bqhd->bkhd', weights, grad_blocks, precision=lax.Precisi...  25 us
    reshape x1, local copies, waits for them, and re-layouts, student_backward(): key_grad.reshape(blocks * NSEL, BS, width)  21.8 us
    reshape x1, local copies, waits for them, and re-layouts, student_backward(): value_grad.reshape(blocks * NSEL, BS, width)  21.6 us
  transfers between devices with their start and end apart: 12, of which 4 were waited for; matrix products, arithmetic and copies ran while one was open for 42% of the time, Pallas kernels for 0%

commit v1 on v0

v1 whole, which is shorter than its diff:
```python
import functools

import jax
import jax.numpy as jnp
from jax import lax
from jax.experimental import pallas as pl
from jax.experimental.pallas import tpu as pltpu
from jax.sharding import PartitionSpec as P

HD = 128
BS = 64
SCALE = HD ** (-0.5)
LOG2E = 1.4426950408889634
MASKED = -1e30
VMEM_LIMIT = 56 * 1024 * 1024

NT = (((1,), (1,)), ((), ()))
TN = (((0,), (0,)), ((), ()))


def dot(a, b, dims=(((1,), (0,)), ((), ()))):
    return lax.dot_general(a, b, dims, preferred_element_type=jnp.float32)


def visible(key_pos, query_pos, first_count):
    low = jnp.where(query_pos < first_count, 0, first_count)
    return (key_pos <= query_pos) & (key_pos >= low)


def teacher_kernel(tile, info_ref, q_ref, k_ref, v_ref, o_ref):
    offset, first_count = info_ref[0], info_ref[1]
    q_tile = q_ref.shape[0]
    q_start = offset + pl.program_id(1) * q_tile
    q_end = q_start + q_tile
    queries = q_ref[...]

    def step(index, carried, masked):
        largest, total, acc = carried
        rows = pl.ds(pl.multiple_of(index * tile, tile), tile)
        scores = dot(k_ref[rows, :], queries, NT)
        if masked:
            key_pos = index * tile + lax.broadcasted_iota(jnp.int32, scores.shape, 0)
            query_pos = q_start + lax.broadcasted_iota(jnp.int32, (1, q_tile), 1)
            scores = jnp.where(visible(key_pos, query_pos, first_count), scores, MASKED)
        new = jnp.maximum(largest, jnp.max(scores, axis=0, keepdims=True))
        weights = jnp.exp2((scores - new) * (SCALE * LOG2E))
        if masked:
            weights = jnp.where(scores > 0.5 * MASKED, weights, 0.0)
        factor = jnp.exp2((largest - new) * (SCALE * LOG2E))
        total = total * factor + jnp.sum(weights, axis=0, keepdims=True)
        acc = acc * factor + dot(v_ref[rows, :], weights.astype(jnp.bfloat16), TN)
        return new, total, acc

    first = jnp.where(q_start >= first_count, first_count // tile, 0)
    last = (q_end + tile - 1) // tile
    straddles = first_count < q_end

    def general(index, carried):
        low, high = index * tile, (index + 1) * tile
        need = (high > q_start) | ((low < first_count) & straddles)
        return lax.cond(
            need,
            lambda c: step(index, c, True),
            lambda c: step(index, c, False),
            carried,
        )

    carried = (
        jnp.full((1, q_tile), MASKED, jnp.float32),
        jnp.zeros((1, q_tile), jnp.float32),
        jnp.zeros((HD, q_tile), jnp.float32),
    )
    _, total, acc = lax.fori_loop(first, last, general, carried)
    o_ref[...] = (acc / total).T.astype(jnp.bfloat16)


def teacher(queries, keys, values, offset, first_count):
    rows, width = queries.shape
    tokens = keys.shape[0]
    heads = width // HD
    tile = 512
    info = jnp.stack([offset, first_count]).astype(jnp.int32)
    return pl.pallas_call(
        functools.partial(teacher_kernel, tile),
        grid_spec=pltpu.PrefetchScalarGridSpec(
            num_scalar_prefetch=1,
            grid=(heads, rows // tile),
            in_specs=[
                pl.BlockSpec((tile, HD), lambda h, i, s: (i, h)),
                pl.BlockSpec((tokens, HD), lambda h, i, s: (0, h)),
                pl.BlockSpec((tokens, HD), lambda h, i, s: (0, h)),
            ],
            out_specs=pl.BlockSpec((tile, HD), lambda h, i, s: (i, h)),
        ),
        out_shape=jax.ShapeDtypeStruct((rows, width), jnp.bfloat16),
        compiler_params=pltpu.CompilerParams(vmem_limit_bytes=VMEM_LIMIT),
        cost_estimate=pl.CostEstimate(
            flops=2 * rows * tokens * width, bytes_accessed=8 * tokens * width, transcendentals=0
        ),
    )(info, queries, keys, values)


def spread(ref, scratch, heads):
    for h in range(heads):
        cols = slice(h * HD, (h + 1) * HD)
        scratch[h * BS : (h + 1) * BS, cols] = ref[:, cols].astype(scratch.dtype)


def student_weights(sel_ref, info_ref, q_wide, k_all, v_all, k_sel, v_sel, pos, heads):
    block = pl.program_id(0)
    count = sel_ref.shape[1]
    offset, first_count = info_ref[0], info_ref[1]
    within = lax.broadcasted_iota(jnp.int32, (BS, 1), 0)
    for e in range(count):
        chosen = sel_ref[block, e]
        source = pl.ds(pl.multiple_of(chosen * BS, BS), BS)
        k_sel[e * BS : (e + 1) * BS, :] = k_all[source, :]
        v_sel[e * BS : (e + 1) * BS, :] = v_all[source, :]
        pos[e * BS : (e + 1) * BS, :] = jnp.broadcast_to(chosen * BS + within, (BS, heads * BS))
    lane = lax.broadcasted_iota(jnp.int32, (1, heads * BS), 1)
    query_pos = offset + block * BS + lax.rem(lane, BS)
    scores = dot(k_sel[...], q_wide[...], NT)
    allowed = visible(pos[...], query_pos, first_count)
    scores = jnp.where(allowed, scores, MASKED)
    largest = jnp.max(scores, axis=0, keepdims=True)
    weights = jnp.exp2((scores - largest) * (SCALE * LOG2E))
    weights = jnp.where(allowed, weights, 0.0)
    return weights, jnp.sum(weights, axis=0, keepdims=True)


def forward_kernel(heads, sel_ref, info_ref, q_ref, k_all, v_all, o_ref, q_wide, k_sel, v_sel, pos):
    @pl.when(pl.program_id(0) == 0)
    def _():
        q_wide[...] = jnp.zeros_like(q_wide)

    spread(q_ref, q_wide, heads)
    weights, total = student_weights(
        sel_ref, info_ref, q_wide, k_all, v_all, k_sel, v_sel, pos, heads
    )
    weights = (weights / total).astype(jnp.bfloat16)
    blended = dot(weights, v_sel[...], TN)
    for h in range(heads):
        cols = slice(h * HD, (h + 1) * HD)
        o_ref[:, cols] = blended[h * BS : (h + 1) * BS, cols].astype(jnp.bfloat16)


def backward_kernel(
    heads, sel_ref, info_ref, q_ref, g_ref, k_all, v_all, dq_ref, dk_ref, dv_ref,
    q_wide, g_wide, k_sel, v_sel, pos,
):
    @pl.when(pl.program_id(0) == 0)
    def _():
        q_wide[...] = jnp.zeros_like(q_wide)
        g_wide[...] = jnp.zeros_like(g_wide)
        dk_ref[...] = jnp.zeros_like(dk_ref)
        dv_ref[...] = jnp.zeros_like(dv_ref)

    spread(q_ref, q_wide, heads)
    spread(g_ref, g_wide, heads)
    weights, total = student_weights(
        sel_ref, info_ref, q_wide, k_all, v_all, k_sel, v_sel, pos, heads
    )
    weights = weights / total
    weight_grad = dot(v_sel[...], g_wide[...], NT)
    row_dots = jnp.sum(weights * weight_grad, axis=0, keepdims=True)
    score_grad = (weights * (weight_grad - row_dots) * SCALE).astype(jnp.bfloat16)
    query_grad = dot(score_grad, k_sel[...], TN)
    for h in range(heads):
        cols = slice(h * HD, (h + 1) * HD)
        dq_ref[:, cols] = query_grad[h * BS : (h + 1) * BS, cols]
    key_grad = dot(score_grad, q_wide[...])
    value_grad = dot(weights.astype(jnp.bfloat16), g_wide[...])
    block = pl.program_id(0)
    for e in range(sel_ref.shape[1]):
        target = pl.ds(pl.multiple_of(sel_ref[block, e] * BS, BS), BS)
        dk_ref[target, :] += key_grad[e * BS : (e + 1) * BS, :]
        dv_ref[target, :] += value_grad[e * BS : (e + 1) * BS, :]


def student_scratch(heads, keys, wides):
    width = heads * HD
    return [pltpu.VMEM((heads * BS, width), jnp.bfloat16)] * wides + [
        pltpu.VMEM((keys, width), jnp.bfloat16),
        pltpu.VMEM((keys, width), jnp.bfloat16),
        pltpu.VMEM((keys, heads * BS), jnp.int32),
    ]


def student_forward(selection, info, queries, keys, values):
    rows, width = queries.shape
    tokens = keys.shape[0]
    heads = width // HD
    row_block = pl.BlockSpec((BS, width), lambda b, *_: (b, 0))
    whole = pl.BlockSpec((tokens, width), lambda b, *_: (0, 0))
    return pl.pallas_call(
        functools.partial(forward_kernel, heads),
        grid_spec=pltpu.PrefetchScalarGridSpec(
            num_scalar_prefetch=2,
            grid=(rows // BS,),
            in_specs=[row_block, whole, whole],
            out_specs=row_block,
            scratch_shapes=student_scratch(heads, selection.shape[1] * BS, 1),
        ),
        out_shape=jax.ShapeDtypeStruct((rows, width), jnp.bfloat16),
        compiler_params=pltpu.CompilerParams(vmem_limit_bytes=VMEM_LIMIT),
        cost_estimate=pl.CostEstimate(
            flops=16 * rows * tokens * width, bytes_accessed=4 * tokens * width, transcendentals=0
        ),
    )(selection, info, queries, keys, values)


def student_backward(selection, info, queries, grads, keys, values):
    rows, width = queries.shape
    tokens = keys.shape[0]
    heads = width // HD
    row_block = pl.BlockSpec((BS, width), lambda b, *_: (b, 0))
    whole = pl.BlockSpec((tokens, width), lambda b, *_: (0, 0))
    return pl.pallas_call(
        functools.partial(backward_kernel, heads),
        grid_spec=pltpu.PrefetchScalarGridSpec(
            num_scalar_prefetch=2,
            grid=(rows // BS,),
            in_specs=[row_block, row_block, whole, whole],
            out_specs=[row_block, whole, whole],
            scratch_shapes=student_scratch(heads, selection.shape[1] * BS, 2),
        ),
        out_shape=[
            jax.ShapeDtypeStruct((rows, width), jnp.float32),
            jax.ShapeDtypeStruct((tokens, width), jnp.float32),
            jax.ShapeDtypeStruct((tokens, width), jnp.float32),
        ],
        compiler_params=pltpu.CompilerParams(vmem_limit_bytes=VMEM_LIMIT),
    )(selection, info, queries, grads, keys, values)


def project_kernel(s_attn, t_attn, s_out, t_out, o_ref):
    o_ref[0] = (dot(s_attn[...], s_out[...]) - dot(t_attn[...], t_out[...])).astype(jnp.bfloat16)


def project(s_attn, t_attn, s_out, t_out, groups):
    rows = s_attn.shape[0]
    model = s_out.shape[1]
    tile = model // groups
    return pl.pallas_call(
        project_kernel,
        grid=(groups,),
        in_specs=[
            pl.BlockSpec(s_attn.shape, lambda j: (0, 0)),
            pl.BlockSpec(t_attn.shape, lambda j: (0, 0)),
            pl.BlockSpec((s_out.shape[0], tile), lambda j: (0, j)),
            pl.BlockSpec((t_out.shape[0], tile), lambda j: (0, j)),
        ],
        out_specs=pl.BlockSpec((1, rows, tile), lambda j: (j, 0, 0)),
        out_shape=jax.ShapeDtypeStruct((groups, rows, tile), jnp.bfloat16),
        compiler_params=pltpu.CompilerParams(vmem_limit_bytes=VMEM_LIMIT),
    )(s_attn, t_attn, s_out, t_out)


def gradient_kernel(m_ref, w_ref, o_ref):
    part = dot(m_ref[0], w_ref[...], NT)

    @pl.when(pl.program_id(0) == 0)
    def _():
        o_ref[...] = part

    @pl.when(pl.program_id(0) > 0)
    def _():
        o_ref[...] += part


def gradient(mismatch, s_out):
    groups, rows, tile = mismatch.shape
    width = s_out.shape[0]
    return pl.pallas_call(
        gradient_kernel,
        grid=(groups,),
        in_specs=[
            pl.BlockSpec((1, rows, tile), lambda j: (j, 0, 0)),
            pl.BlockSpec((width, tile), lambda j: (0, j)),
        ],
        out_specs=pl.BlockSpec((rows, width), lambda j: (0, 0)),
        out_shape=jax.ShapeDtypeStruct((rows, width), jnp.float32),
        compiler_params=pltpu.CompilerParams(vmem_limit_bytes=VMEM_LIMIT),
    )(mismatch, s_out)


def on_device(t_query, t_key, t_value, t_out, s_query, s_key, s_value, s_out, segments, selection):
    row_count = t_query.shape[0]
    heads = t_query.shape[1] // HD
    cycle = lax.axis_size("blk")
    groups = lax.axis_size("head") * lax.axis_size("grp")
    my_index = lax.axis_index("blk")
    first_row = my_index * row_count

    first_count = lax.psum(jnp.sum((segments == 0).astype(jnp.int32)), "blk")
    info = jnp.stack([first_row, first_count]).astype(jnp.int32)

    if heads % cycle == 0:
        def by_head(rows):
            return lax.all_to_all(rows, "blk", split_axis=1, concat_axis=0, tiled=True)

        whole_heads = teacher(
            by_head(t_query), by_head(t_key), by_head(t_value), jnp.int32(0), first_count
        )
        t_attn = lax.all_to_all(whole_heads, "blk", split_axis=0, concat_axis=1, tiled=True)
    else:
        t_attn = teacher(
            t_query,
            lax.all_gather(t_key, "blk", axis=0, tiled=True),
            lax.all_gather(t_value, "blk", axis=0, tiled=True),
            first_row,
            first_count,
        )

    key_full = lax.all_gather(s_key, "blk", axis=0, tiled=True)
    value_full = lax.all_gather(s_value, "blk", axis=0, tiled=True)
    s_attn = student_forward(selection, info, s_query, key_full, value_full)

    terms = project(s_attn, t_attn, s_out, t_out, groups)
    mismatch = lax.psum_scatter(terms, ("head", "grp"), scatter_dimension=0, tiled=False)
    grad_attn = gradient(lax.all_gather(mismatch, ("head", "grp"), axis=0, tiled=False), s_out)
    grad_query, grad_keys, grad_values = student_backward(
        selection, info, s_query, grad_attn, key_full, value_full
    )

    def own(full, index):
        return lax.dynamic_slice_in_dim(full, index * row_count, row_count, 0)

    key_grads, value_grads = own(grad_keys, my_index), own(grad_values, my_index)
    for distance in range(1, cycle):
        owner = jnp.maximum(my_index - distance, 0)
        route = [(i, i - distance) for i in range(distance, cycle)]
        for_keys = lax.ppermute(own(grad_keys, owner).astype(jnp.bfloat16), "blk", route)
        for_values = lax.ppermute(own(grad_values, owner).astype(jnp.bfloat16), "blk", route)
        key_grads = key_grads + for_keys.astype(jnp.float32)
        value_grads = value_grads + for_values.astype(jnp.float32)
    return (mismatch.astype(jnp.float32), grad_query, key_grads, value_grads)


def solution(mesh):
    split = ("head", "grp")
    tokens, weights = P("blk", split), P(split, None)
    return jax.shard_map(
        on_device,
        mesh=mesh,
        in_specs=(
            tokens, tokens, tokens, weights, tokens, tokens, tokens, weights, P("blk"),
            P("blk", None),
        ),
        out_specs=(tokens,) * 4,
        check_vma=False,
    )
```

time: 820 us -> 433 us (0.53); the launches traced: 808 us -> 430 us
  local copies, waits for them, and re-layouts: 265 us -> 11.3 us
  other arithmetic: 140 us -> 9.89 us
  matrix products: 117 us -> 0 us
  Pallas kernels: 0 us -> 97.8 us
  starting transfers between devices: 7.97 us -> 23.6 us
  waiting for transfers between devices: 246 us -> 261 us
    gather x8 -> x0, local copies, waits for them, and re-layouts: 136 us -> none  [the longest x2 90.6 us: student_forward(): key_seg = segment_all[key_pos]]
    dot_general x13 -> x0, matrix products: 117 us -> none  [the longest x1 19.1 us: student_backward(): jnp.einsum('bhqk,bqhd->bkhd', weights, grad_blocks, precision=lax.Precisi...]
    scatter-add x2 -> x0, other arithmetic: 104 us -> none  [the longest x1 52.3 us: student_backward(): value_total = jnp.zeros((token_count // BS, BS, width), jnp.float32).at[f...]
    pallas_call x0 -> x5, Pallas kernels: none -> 97.8 us  [the longest x1 29.2 us: teacher(): pl.pallas_call(functools.partial(teacher_kernel, tile), grid_spec=pltpu.P...]
    reduce_scatter x1, waiting for transfers between devices: 155 us -> 91.5 us  [on_device(): lax.psum_scatter(terms, ('head', 'grp'), scatter_dimension=0, tiled=False)]
    reshape x9 -> x0, local copies, waits for them, and re-layouts: 62.1 us -> none  [the longest x1 21.8 us: student_backward(): key_grad.reshape(blocks * NSEL, BS, width)]
    all_to_all x0 -> x4, waiting for transfers between devices: none -> 48.3 us  [the longest x3 40.2 us: by_head(): return lax.all_to_all(rows, 'blk', split_axis=1, concat_axis=0, tiled=True)]
    transpose x3 -> x0, local copies, waits for them, and re-layouts: 40.2 us -> none  [the longest x1 25 us: student_backward(): jnp.einsum('bhqk,bqhd->bkhd', weights, grad_blocks, precision=lax.Precisi...]
  transfers between devices with their start and end apart: 12 -> 14, of which waited for: 4 -> 8; matrix products, arithmetic and copies ran while one was open for 42% -> 3% of each run, Pallas kernels for 0% -> 7%
where the time goes in v1:
time: 433 us; the launch traced here: 430 us
  waiting for transfers between devices  261 us (60%)
  Pallas kernels  97.8 us (23%)
  starting transfers between devices  23.6 us (5%)
  between operations  13.9 us (3%)
  blocking collectives  12.6 us (3%)
  local copies, waits for them, and re-layouts  11.3 us (3%)
  other arithmetic  9.89 us (2%)
    reduce_scatter x1, waiting for transfers between devices, on_device(): lax.psum_scatter(terms, ('head', 'grp'), scatter_dimension=0, tiled=False)  91.5 us
    all_gather x1, waiting for transfers between devices, on_device(): lax.all_gather(mismatch, ('head', 'grp'), axis=0, tiled=False)  82 us
    all_to_all x3, waiting for transfers between devices, by_head(): return lax.all_to_all(rows, 'blk', split_axis=1, concat_axis=0, tiled=True)  40.2 us
    pallas_call x1, Pallas kernels, teacher(): pl.pallas_call(functools.partial(teacher_kernel, tile), grid_spec=pltpu.P...  29.2 us
    pallas_call x1, Pallas kernels, student_backward(): pl.pallas_call(functools.partial(backward_kernel, heads), grid_spec=pltpu...  28.5 us
    ppermute x3, waiting for transfers between devices, on_device(): lax.ppermute(own(grad_keys, owner).astype(jnp.bfloat16), 'blk', route)  18.8 us
    pallas_call x1, Pallas kernels, student_forward(): pl.pallas_call(functools.partial(forward_kernel, heads), grid_spec=pltpu....  18.6 us
    ppermute x3, waiting for transfers between devices, on_device(): lax.ppermute(own(grad_values, owner).astype(jnp.bfloat16), 'blk', route)  18.6 us
  transfers between devices with their start and end apart: 14, of which 8 were waited for; matrix products, arithmetic and copies ran while one was open for 3% of the time, Pallas kernels for 7%

profile of v1, /device:TPU:0, one launch (start us, length us, event | category | flops | bytes accessed | tf_op | source)
XLA Modules:
  0.0 429.6 jit_solution(2215288019594050590)
XLA Ops:
  7.2 0.0 copy-start
  7.2 0.0 all-gather.4.cloned.1.call-start
  7.2 0.7 all-gather.4.cloned.1.call-update
  7.9 0.5 copy-done
  8.4 1.1 copy_bitcast_fusion.3
  9.5 5.2 %all-to-all-start = ((bf16[1024,4,128]{2,0,1:T(8,128)(2,1)}), bf16[1024,4,128]{2,0,1:T(8,128)(2,1)}, u32[]{:S(2)}, u32[]{:S(2)}) async-start(bf16[1024,4,128]{2,0,1:T(8,128)(2,1)} %copy_bitcast_fusion.3), calls=%async_computation | async-start | bytes 2097152 | tf_op jit(solution)/shard_map/all_to_all | solution.py:300
  14.7 0.7 all-gather.6.cloned.1.call-update
  15.5 0.0 copy-start.6
  15.5 1.2 copy_bitcast_fusion.2
  16.6 18.0 %all-to-all-done = bf16[1024,4,128]{2,0,1:T(8,128)(2,1)} async-done(((bf16[1024,4,128]{2,0,1:T(8,128)(2,1)}), bf16[1024,4,128]{2,0,1:T(8,128)(2,1)}, u32[]{:S(2)}, u32[]{:S(2)}) %all-to-all-start) | async-done | bytes 1048608 | tf_op jit(solution)/shard_map/all_to_all | solution.py:300
  34.6 3.5 all-to-all-start.1
  38.2 1.2 copy_bitcast_fusion.1
  39.3 22.2 %all-to-all-done.1 = bf16[1024,4,128]{2,0,1:T(8,128)(2,1)S(1)} async-done(((bf16[1024,4,128]{2,0,1:T(8,128)(2,1)}), bf16[1024,4,128]{2,0,1:T(8,128)(2,1)S(1)}, u32[]{:S(2)}, u32[]{:S(2)}) %all-to-all-start.1) | async-done | bytes 1048608 | tf_op jit(solution)/shard_map/all_to_all | solution.py:300
  61.5 3.5 all-to-all-start.2
  65.0 0.6 convert_reduce_fusion
  65.7 12.6 %psum.7 = s32[1]{0:T(128)} all-reduce(s32[1]{0:T(128)} %bitcast.1), channel_id=1, replica_groups=mesh['blk'=4,'head'=4,'grp'=2] {'blk'}, use_global_device_ids=true, to_apply=%region_1.0 | all-reduce | flops 1 | bytes 8 | tf_op jit(solution)/shard_map/psum | solution.py:295
  78.2 1.1 pad_add_fusion.1.info_ref
  79.4 0.0 all-to-all-done.2
  79.4 1.0 copy-done.5
  80.4 29.2 %shard_map.130 = bf16[4096,128]{1,0:T(8,128)(2,1)} custom-call(s32[2]{0:T(128)} %pad_add_fusion.1.info_ref, bf16[4096,128]{1,0:T(8,128)(2,1)} %bitcast.3.q_ref, bf16[4096,128]{1,0:T(8,128)(2,1)} %bitcast.36, bf16[4096,128]{1,0:T(8,128)(2,1)} %bitcast.38), custom_call_target="tpu_custom_call" | custom-call | flops 4294967296 | bytes 4194304 | tf_op jit(solution)/shard_map/pallas_call | solution.py:83
  109.5 3.5 all-to-all-start.3
  113.1 0.0 reduce-scatter.2.cloned.1.call-start
  113.1 1.2 pad_add_fusion.info_ref
  114.3 8.1 %all-to-all-done.3 = bf16[4,1024,128]{2,1,0:T(8,128)(2,1)S(1)} async-done(((bf16[4,1024,128]{2,1,0:T(8,128)(2,1)}), bf16[4,1024,128]{2,1,0:T(8,128)(2,1)S(1)}, u32[]{:S(2)}, u32[]{:S(2)}) %all-to-all-start.3) | async-done | bytes 1048608 | tf_op jit(solution)/shard_map/all_to_all | solution.py:305
  122.5 1.1 copy_bitcast_fusion.t_attn
  123.6 18.6 %shard_map.129.s_attn = bf16[1024,256]{1,0:T(8,128)(2,1)} custom-call(s32[16,16]{1,0:T(8,128)} %sel_ref.3, s32[2]{0:T(128)} %pad_add_fusion.info_ref, bf16[1024,256]{1,0:T(8,128)(2,1)} %q_ref.3, bf16[4096,256]{1,0:T(8,128)(2,1)} %all-gather.4.cloned.1.call-done.k_all, bf16[4096,256]{1,0:T(8,128)(2,1)} %all-gather.6.cloned.1.call-done.v_all), custom_call_target="tpu_custom_call" | custom-call | flops 17179869184 | bytes 4194304 | tf_op jit(solution)/shard_map/pallas_call | solution.py:195
  142.2 12.4 %shard_map.131 = bf16[8,1024,512]{2,1,0:T(8,128)(2,1)} custom-call(bf16[1024,256]{1,0:T(8,128)(2,1)} %shard_map.129.s_attn, bf16[1024,512]{1,0:T(8,128)(2,1)} %copy_bitcast_fusion.t_attn, bf16[256,4096]{1,0:T(8,128)(2,1)} %w_ref.1, bf16[512,4096]{1,0:T(8,128)(2,1)} %t_out.1), custom_call_target="tpu_custom_call" | custom-call | tf_op jit(solution)/shard_map/pallas_call | solution.py:244
  154.5 0.0 reduce-scatter.2.cloned.1.call-update
  154.5 0.0 all-gather.8.cloned.1.call-start
  154.6 91.5 %reduce-scatter.2.cloned.1.call-done = bf16[1,1024,512]{2,1,0:T(8,128)(2,1)} async-done(((bf16[8,1024,512]{2,1,0:T(8,128)(2,1)}), bf16[1,1024,512]{2,1,0:T(8,128)(2,1)}) %reduce-scatter.2.cloned.1.call-update) | async-done | bytes 1048592 | tf_op jit(solution)/shard_map/reduce_scatter | solution.py:320
  246.1 0.0 all-gather.8.cloned.1.call-update
  246.2 82.0 %all-gather.8.cloned.1.call-done.m_ref = bf16[8,1024,512]{2,1,0:T(8,128)(2,1)} async-done(((bf16[1,1024,512]{2,1,0:T(8,128)(2,1)}), bf16[8,1024,512]{2,1,0:T(8,128)(2,1)}) %all-gather.8.cloned.1.call-update) | async-done | bytes 8388624 | tf_op jit(solution)/shard_map/all_gather | solution.py:321
  328.1 9.1 %shard_map.132.g_ref = f32[1024,256]{1,0:T(8,128)} custom-call(bf16[8,1024,512]{2,1,0:T(8,128)(2,1)} %all-gather.8.cloned.1.call-done.m_ref, bf16[256,4096]{1,0:T(8,128)(2,1)} %w_ref.1), custom_call_target="tpu_custom_call" | custom-call | tf_op jit(solution)/shard_map/pallas_call | solution.py:274
  337.3 28.5 %shard_map.133 = (f32[1024,256]{1,0:T(8,128)}, f32[4096,256]{1,0:T(8,128)}, f32[4096,256]{1,0:T(8,128)}) custom-call(s32[16,16]{1,0:T(8,128)} %sel_ref.3, s32[2]{0:T(128)} %pad_add_fusion.info_ref, bf16[1024,256]{1,0:T(8,128)(2,1)} %q_ref.3, f32[1024,256]{1,0:T(8,128)} %shard_map.132.g_ref, bf16[4096,256]{1,0:T(8,128)(2,1)} %all-gather.4.cloned.1.call-done.k_all, ...), custom_call_target="tpu_custom_call" | custom-call | tf_op jit(solution)/shard_map/pallas_call | solution.py:218
  365.7 3.1 dynamic-slice_convert_fusion.2
  368.8 1.3 collective-permute-start.3
  370.1 1.3 collective-permute-start.4
  371.4 1.3 collective-permute-start.5
  372.7 2.3 dynamic-slice_convert_fusion.5
  374.9 1.3 collective-permute-start
  376.2 1.3 collective-permute-start.1
  377.5 8.2 %collective-permute-done.3 = bf16[1024,256]{1,0:T(8,128)(2,1)} collective-permute-done((bf16[1024,256]{1,0:T(8,128)(2,1)}, bf16[1024,256]{1,0:T(8,128)(2,1)}, u32[]{:S(2)}, u32[]{:S(2)}) %collective-permute-start.3) | collective-permute-done | bytes 524320 | tf_op jit(solution)/shard_map/ppermute | solution.py:334
  385.8 1.3 collective-permute-start.2
  387.1 1.6 bitcast_convert_fusion
  388.7 10.3 %collective-permute-done.4 = bf16[1024,256]{1,0:T(8,128)(2,1)} collective-permute-done((bf16[1024,256]{1,0:T(8,128)(2,1)S(1)}, bf16[1024,256]{1,0:T(8,128)(2,1)}, u32[]{:S(2)}, u32[]{:S(2)}) %collective-permute-start.4) | collective-permute-done | bytes 524320 | tf_op jit(solution)/shard_map/ppermute | solution.py:334
  399.0 2.9 convert_add_fusion
  401.9 18.8 %collective-permute-done.1 = bf16[1024,256]{1,0:T(8,128)(2,1)S(1)} collective-permute-done((bf16[1024,256]{1,0:T(8,128)(2,1)S(1)}, bf16[1024,256]{1,0:T(8,128)(2,1)S(1)}, u32[]{:S(2)}, u32[]{:S(2)}) %collective-permute-start.1) | collective-permute-done | bytes 524320 | tf_op jit(solution)/shard_map/ppermute | solution.py:333
  420.7 2.4 convert_add_fusion.1
  (16 shorter events, 0.0 us)
Async XLA Ops:
  7.2 1.2 copy-start
  7.2 8.3 %copy-start.2 = (bf16[1024,512]{1,0:T(8,128)(2,1)S(1)}, bf16[1024,512]{1,0:T(8,128)(2,1)}, u32[]{:S(2)}) copy-start(bf16[1024,512]{1,0:T(8,128)(2,1)} %param.11) | copy-start | bytes 3145732
  7.2 116.4 %all-gather.4.cloned.1.call-start = ((), (), s32[]{:S(2)}) async-start(), calls=%async_computation.5 | async-start | bytes 2621440 | tf_op jit(solution)/shard_map/all_gather | solution.py:315
  8.4 29.8 %copy-start.3 = (bf16[1024,512]{1,0:T(8,128)(2,1)S(1)}, bf16[1024,512]{1,0:T(8,128)(2,1)}, u32[]{:S(2)}) copy-start(bf16[1024,512]{1,0:T(8,128)(2,1)} %param.12) | copy-start | bytes 3145732
  9.5 25.1 %all-to-all-start = ((bf16[1024,4,128]{2,0,1:T(8,128)(2,1)}), bf16[1024,4,128]{2,0,1:T(8,128)(2,1)}, u32[]{:S(2)}, u32[]{:S(2)}) async-start(bf16[1024,4,128]{2,0,1:T(8,128)(2,1)} %copy_bitcast_fusion.3), calls=%async_computation | async-start | bytes 2097152 | tf_op jit(solution)/shard_map/all_to_all | solution.py:300
  14.7 108.8 %all-gather.6.cloned.1.call-start = ((), (), s32[]{:S(2)}) async-start(), calls=%async_computation.6 | async-start | bytes 2621440 | tf_op jit(solution)/shard_map/all_gather | solution.py:316
  15.5 49.5 %copy-start.6 = (s32[1024]{0:T(1024)S(1)}, s32[1024]{0:T(1024)}, u32[]{:S(2)}) copy-start(s32[1024]{0:T(1024)} %param.18) | copy-start | bytes 12292
  34.6 26.9 %all-to-all-start.1 = ((bf16[1024,4,128]{2,0,1:T(8,128)(2,1)}), bf16[1024,4,128]{2,0,1:T(8,128)(2,1)S(1)}, u32[]{:S(2)}, u32[]{:S(2)}) async-start(bf16[1024,4,128]{2,0,1:T(8,128)(2,1)} %copy_bitcast_fusion.2), calls=%async_computation.1 | async-start | bytes 2097152 | tf_op jit(solution)/shard_map/all_to_all | solution.py:300
  61.5 17.9 %copy-start.4 = (bf16[1024,4,128]{2,0,1:T(8,128)(2,1)}, bf16[1024,4,128]{2,0,1:T(8,128)(2,1)S(1)}, u32[]{:S(2)}) copy-start(bf16[1024,4,128]{2,0,1:T(8,128)(2,1)S(1)} %all-to-all-done.1) | copy-start | bytes 3145732
  61.5 17.9 %all-to-all-start.2 = ((bf16[1024,4,128]{2,0,1:T(8,128)(2,1)}), bf16[1024,4,128]{2,0,1:T(8,128)(2,1)S(1)}, u32[]{:S(2)}, u32[]{:S(2)}) async-start(bf16[1024,4,128]{2,0,1:T(8,128)(2,1)} %copy_bitcast_fusion.1), calls=%async_computation.2 | async-start | bytes 2097152 | tf_op jit(solution)/shard_map/all_to_all | solution.py:300
  79.4 1.0 copy-start.5
  109.5 12.9 %all-to-all-start.3 = ((bf16[4,1024,128]{2,1,0:T(8,128)(2,1)}), bf16[4,1024,128]{2,1,0:T(8,128)(2,1)S(1)}, u32[]{:S(2)}, u32[]{:S(2)}) async-start(bf16[4,1024,128]{2,1,0:T(8,128)(2,1)} %bitcast.37), calls=%async_computation.3 | async-start | bytes 2097152 | tf_op jit(solution)/shard_map/all_to_all | solution.py:305
  113.1 133.1 %reduce-scatter.2.cloned.1.call-start = ((), (), s32[]{:S(2)}) async-start(), calls=%async_computation.7 | async-start | bytes 9437184 | tf_op jit(solution)/shard_map/reduce_scatter | solution.py:320
  154.5 173.6 %all-gather.8.cloned.1.call-start = ((), (), s32[]{:S(2)}) async-start(), calls=%async_computation.8 | async-start | bytes 9437184 | tf_op jit(solution)/shard_map/all_gather | solution.py:321
  365.7 21.4 %copy-start.1 = (bf16[1,1024,512]{2,1,0:T(8,128)(2,1)S(1)}, bf16[1,1024,512]{2,1,0:T(8,128)(2,1)}, u32[]{:S(2)}) copy-start(bf16[1,1024,512]{2,1,0:T(8,128)(2,1)} %reduce-scatter.2.cloned.1.call-done) | copy-start | bytes 3145732
  368.8 17.0 %collective-permute-start.3 = (bf16[1024,256]{1,0:T(8,128)(2,1)}, bf16[1024,256]{1,0:T(8,128)(2,1)}, u32[]{:S(2)}, u32[]{:S(2)}) collective-permute-start(bf16[1024,256]{1,0:T(8,128)(2,1)} %get-tuple-element.10), channel_id=1, source_target_pairs={{8,0},{16,8},{24,16},{9,1},{17,9},{25,17},{10,2},{18,10},{26,18},{... | collective-permute-start | bytes 1572872 | tf_op jit(solution)/shard_map/ppermute | solution.py:334
  370.1 28.9 %collective-permute-start.4 = (bf16[1024,256]{1,0:T(8,128)(2,1)S(1)}, bf16[1024,256]{1,0:T(8,128)(2,1)}, u32[]{:S(2)}, u32[]{:S(2)}) collective-permute-start(bf16[1024,256]{1,0:T(8,128)(2,1)S(1)} %get-tuple-element.12), channel_id=1, source_target_pairs={{16,0},{24,8},{17,1},{25,9},{18,2},{26,10},{19,3},{27,11},{20,4},{... | collective-permute-start | bytes 1572872 | tf_op jit(solution)/shard_map/ppermute | solution.py:334
  371.4 27.6 %collective-permute-start.5 = (bf16[1024,256]{1,0:T(8,128)(2,1)S(1)}, bf16[1024,256]{1,0:T(8,128)(2,1)}, u32[]{:S(2)}, u32[]{:S(2)}) collective-permute-start(bf16[1024,256]{1,0:T(8,128)(2,1)S(1)} %get-tuple-element.11), channel_id=1, source_target_pairs={{24,0},{25,1},{26,2},{27,3},{28,4},{29,5},{30,6},{31,7}} | collective-permute-start | bytes 1572872 | tf_op jit(solution)/shard_map/ppermute | solution.py:334
  374.9 26.9 %collective-permute-start = (bf16[1024,256]{1,0:T(8,128)(2,1)S(1)}, bf16[1024,256]{1,0:T(8,128)(2,1)S(1)}, u32[]{:S(2)}, u32[]{:S(2)}) collective-permute-start(bf16[1024,256]{1,0:T(8,128)(2,1)S(1)} %get-tuple-element.13), channel_id=1, source_target_pairs={{8,0},{16,8},{24,16},{9,1},{17,9},{25,17},{10,2},{18,10},{26,18},{... | collective-permute-start | bytes 1572872 | tf_op jit(solution)/shard_map/ppermute | solution.py:333
  376.2 44.4 %collective-permute-start.1 = (bf16[1024,256]{1,0:T(8,128)(2,1)S(1)}, bf16[1024,256]{1,0:T(8,128)(2,1)S(1)}, u32[]{:S(2)}, u32[]{:S(2)}) collective-permute-start(bf16[1024,256]{1,0:T(8,128)(2,1)S(1)} %get-tuple-element.15), channel_id=1, source_target_pairs={{16,0},{24,8},{17,1},{25,9},{18,2},{26,10},{19,3},{27,11},{20,4},{... | collective-permute-start | bytes 1572872 | tf_op jit(solution)/shard_map/ppermute | solution.py:333
  385.8 34.9 %collective-permute-start.2 = (bf16[1024,256]{1,0:T(8,128)(2,1)S(1)}, bf16[1024,256]{1,0:T(8,128)(2,1)S(1)}, u32[]{:S(2)}, u32[]{:S(2)}) collective-permute-start(bf16[1024,256]{1,0:T(8,128)(2,1)S(1)} %get-tuple-element.14), channel_id=1, source_target_pairs={{24,0},{25,1},{26,2},{27,3},{28,4},{29,5},{30,6},{31,7}} | collective-permute-start | bytes 1572872 | tf_op jit(solution)/shard_map/ppermute | solution.py:333
Sparse Core Ops, SparseCore 0:
  9.8 52.8 all-gather.3
  64.6 35.8 all-gather.5
  154.7 91.4 reduce-scatter.1
  247.6 80.4 all-gather.7

commit v2 on v1

--- a/solution.py
+++ b/solution.py
@@ -106,14 +106,14 @@
         scratch[h * BS : (h + 1) * BS, cols] = ref[:, cols].astype(scratch.dtype)
 
 
-def student_weights(sel_ref, info_ref, q_wide, k_all, v_all, k_sel, v_sel, pos, heads):
+def student_weights(sel_ref, place_ref, info_ref, q_wide, k_all, v_all, k_sel, v_sel, pos, heads):
     block = pl.program_id(0)
     count = sel_ref.shape[1]
     offset, first_count = info_ref[0], info_ref[1]
     within = lax.broadcasted_iota(jnp.int32, (BS, 1), 0)
     for e in range(count):
         chosen = sel_ref[block, e]
-        source = pl.ds(pl.multiple_of(chosen * BS, BS), BS)
+        source = pl.ds(pl.multiple_of(place_ref[block, e] * BS, BS), BS)
         k_sel[e * BS : (e + 1) * BS, :] = k_all[source, :]
         v_sel[e * BS : (e + 1) * BS, :] = v_all[source, :]
         pos[e * BS : (e + 1) * BS, :] = jnp.broadcast_to(chosen * BS + within, (BS, heads * BS))
@@ -128,14 +128,14 @@
     return weights, jnp.sum(weights, axis=0, keepdims=True)
 
 
-def forward_kernel(heads, sel_ref, info_ref, q_ref, k_all, v_all, o_ref, q_wide, k_sel, v_sel, pos):
+def forward_kernel(heads, sel_ref, place_ref, info_ref, q_ref, k_all, v_all, o_ref, q_wide, k_sel, v_sel, pos):
     @pl.when(pl.program_id(0) == 0)
     def _():
         q_wide[...] = jnp.zeros_like(q_wide)
 
     spread(q_ref, q_wide, heads)
     weights, total = student_weights(
-        sel_ref, info_ref, q_wide, k_all, v_all, k_sel, v_sel, pos, heads
+        sel_ref, place_ref, info_ref, q_wide, k_all, v_all, k_sel, v_sel, pos, heads
     )
     weights = (weights / total).astype(jnp.bfloat16)
     blended = dot(weights, v_sel[...], TN)
@@ -145,20 +145,23 @@
 
 
 def backward_kernel(
-    heads, sel_ref, info_ref, q_ref, g_ref, k_all, v_all, dq_ref, dk_ref, dv_ref,
-    q_wide, g_wide, k_sel, v_sel, pos,
+    heads, cycle, sel_ref, place_ref, info_ref, q_ref, g_ref, k_all, v_all, dq_ref, *rest
 ):
-    @pl.when(pl.program_id(0) == 0)
+    own_ref, far_refs = rest[0], rest[1:cycle]
+    dk_sum, dv_sum, q_wide, g_wide, k_sel, v_sel, pos = rest[cycle:]
+    block = pl.program_id(0)
+
+    @pl.when(block == 0)
     def _():
         q_wide[...] = jnp.zeros_like(q_wide)
         g_wide[...] = jnp.zeros_like(g_wide)
-        dk_ref[...] = jnp.zeros_like(dk_ref)
-        dv_ref[...] = jnp.zeros_like(dv_ref)
+        dk_sum[...] = jnp.zeros_like(dk_sum)
+        dv_sum[...] = jnp.zeros_like(dv_sum)
 
     spread(q_ref, q_wide, heads)
     spread(g_ref, g_wide, heads)
     weights, total = student_weights(
-        sel_ref, info_ref, q_wide, k_all, v_all, k_sel, v_sel, pos, heads
+        sel_ref, place_ref, info_ref, q_wide, k_all, v_all, k_sel, v_sel, pos, heads
     )
     weights = weights / total
     weight_grad = dot(v_sel[...], g_wide[...], NT)
@@ -170,11 +173,19 @@
         dq_ref[:, cols] = query_grad[h * BS : (h + 1) * BS, cols]
     key_grad = dot(score_grad, q_wide[...])
     value_grad = dot(weights.astype(jnp.bfloat16), g_wide[...])
-    block = pl.program_id(0)
     for e in range(sel_ref.shape[1]):
-        target = pl.ds(pl.multiple_of(sel_ref[block, e] * BS, BS), BS)
-        dk_ref[target, :] += key_grad[e * BS : (e + 1) * BS, :]
-        dv_ref[target, :] += value_grad[e * BS : (e + 1) * BS, :]
+        target = pl.ds(pl.multiple_of(place_ref[block, e] * BS, BS), BS)
+        dk_sum[target, :] += key_grad[e * BS : (e + 1) * BS, :]
+        dv_sum[target, :] += value_grad[e * BS : (e + 1) * BS, :]
+
+    @pl.when(block == pl.num_programs(0) - 1)
+    def _():
+        rows = own_ref.shape[1]
+        own_ref[0] = dk_sum[:rows, :]
+        own_ref[1] = dv_sum[:rows, :]
+        for d in range(1, cycle):
+            far_refs[d - 1][0] = dk_sum[d * rows : (d + 1) * rows, :].astype(jnp.bfloat16)
+            far_refs[d - 1][1] = dv_sum[d * rows : (d + 1) * rows, :].astype(jnp.bfloat16)
 
 
 def student_scratch(heads, keys, wides):
@@ -186,7 +197,7 @@
     ]
 
 
-def student_forward(selection, info, queries, keys, values):
+def student_forward(tables, queries, keys, values):
     rows, width = queries.shape
     tokens = keys.shape[0]
     heads = width // HD
@@ -195,42 +206,48 @@
     return pl.pallas_call(
         functools.partial(forward_kernel, heads),
         grid_spec=pltpu.PrefetchScalarGridSpec(
-            num_scalar_prefetch=2,
+            num_scalar_prefetch=3,
             grid=(rows // BS,),
             in_specs=[row_block, whole, whole],
             out_specs=row_block,
-            scratch_shapes=student_scratch(heads, selection.shape[1] * BS, 1),
+            scratch_shapes=student_scratch(heads, tables[0].shape[1] * BS, 1),
         ),
         out_shape=jax.ShapeDtypeStruct((rows, width), jnp.bfloat16),
         compiler_params=pltpu.CompilerParams(vmem_limit_bytes=VMEM_LIMIT),
         cost_estimate=pl.CostEstimate(
             flops=16 * rows * tokens * width, bytes_accessed=4 * tokens * width, transcendentals=0
         ),
-    )(selection, info, queries, keys, values)
-
-
-def student_backward(selection, info, queries, grads, keys, values):
+    )(*tables, queries, keys, values)
+
+
+def student_backward(tables, queries, grads, keys, values):
     rows, width = queries.shape
     tokens = keys.shape[0]
+    cycle = tokens // rows
     heads = width // HD
     row_block = pl.BlockSpec((BS, width), lambda b, *_: (b, 0))
     whole = pl.BlockSpec((tokens, width), lambda b, *_: (0, 0))
+    pair = pl.BlockSpec((2, rows, width), lambda b, *_: (0, 0, 0))
     return pl.pallas_call(
-        functools.partial(backward_kernel, heads),
+        functools.partial(backward_kernel, heads, cycle),
         grid_spec=pltpu.PrefetchScalarGridSpec(
-            num_scalar_prefetch=2,
+            num_scalar_prefetch=3,
             grid=(rows // BS,),
             in_specs=[row_block, row_block, whole, whole],
-            out_specs=[row_block, whole, whole],
-            scratch_shapes=student_scratch(heads, selection.shape[1] * BS, 2),
+            out_specs=[row_block] + [pair] * cycle,
+            scratch_shapes=[pltpu.VMEM((tokens, width), jnp.float32)] * 2
+            + student_scratch(heads, tables[0].shape[1] * BS, 2),
         ),
         out_shape=[
             jax.ShapeDtypeStruct((rows, width), jnp.float32),
-            jax.ShapeDtypeStruct((tokens, width), jnp.float32),
-            jax.ShapeDtypeStruct((tokens, width), jnp.float32),
-        ],
+            jax.ShapeDtypeStruct((2, rows, width), jnp.float32),
+        ]
+        + [jax.ShapeDtypeStruct((2, rows, width), jnp.bfloat16)] * (cycle - 1),
         compiler_params=pltpu.CompilerParams(vmem_limit_bytes=VMEM_LIMIT),
-    )(selection, info, queries, grads, keys, values)
+        cost_estimate=pl.CostEstimate(
+            flops=32 * rows * tokens * width, bytes_accessed=8 * tokens * width, transcendentals=0
+        ),
+    )(*tables, queries, grads, keys, values)
 
 
 def project_kernel(s_attn, t_attn, s_out, t_out, o_ref):
@@ -256,44 +273,35 @@
     )(s_attn, t_attn, s_out, t_out)
 
 
-def gradient_kernel(m_ref, w_ref, o_ref):
-    part = dot(m_ref[0], w_ref[...], NT)
-
-    @pl.when(pl.program_id(0) == 0)
-    def _():
-        o_ref[...] = part
-
-    @pl.when(pl.program_id(0) > 0)
-    def _():
-        o_ref[...] += part
-
-
-def gradient(mismatch, s_out):
-    groups, rows, tile = mismatch.shape
-    width = s_out.shape[0]
-    return pl.pallas_call(
-        gradient_kernel,
-        grid=(groups,),
-        in_specs=[
-            pl.BlockSpec((1, rows, tile), lambda j: (j, 0, 0)),
-            pl.BlockSpec((width, tile), lambda j: (0, j)),
-        ],
-        out_specs=pl.BlockSpec((rows, width), lambda j: (0, 0)),
-        out_shape=jax.ShapeDtypeStruct((rows, width), jnp.float32),
-        compiler_params=pltpu.CompilerParams(vmem_limit_bytes=VMEM_LIMIT),
-    )(mismatch, s_out)
+def from_earlier(rows, distance):
+    route = [(i - distance, i) for i in range(distance, lax.axis_size("blk"))]
+    return lax.ppermute(rows, "blk", route)
 
 
 def on_device(t_query, t_key, t_value, t_out, s_query, s_key, s_value, s_out, segments, selection):
     row_count = t_query.shape[0]
     heads = t_query.shape[1] // HD
     cycle = lax.axis_size("blk")
+    split = ("head", "grp")
     groups = lax.axis_size("head") * lax.axis_size("grp")
     my_index = lax.axis_index("blk")
     first_row = my_index * row_count
-
-    first_count = lax.psum(jnp.sum((segments == 0).astype(jnp.int32)), "blk")
+    shard_blocks = row_count // BS
+
+    count = jnp.sum((segments == 0).astype(jnp.int32)).reshape(1)
+    first_count = count
+    for distance in range(1, cycle):
+        route = [(i, (i + distance) % cycle) for i in range(cycle)]
+        first_count = first_count + lax.ppermute(count, "blk", route)
+    first_count = first_count[0]
     info = jnp.stack([first_row, first_count]).astype(jnp.int32)
+
+    mixed = []
+    for h in range(s_out.shape[0] // HD):
+        part = lax.all_gather(s_out[h * HD : (h + 1) * HD, :], split, axis=0, tiled=True)
+        mixed.append(
+            (dot(s_out, part, NT).astype(jnp.bfloat16), dot(t_out, part, NT).astype(jnp.bfloat16))
+        )
 
     if heads % cycle == 0:
         def by_head(rows):
@@ -312,29 +320,27 @@
             first_count,
         )
 
-    key_full = lax.all_gather(s_key, "blk", axis=0, tiled=True)
-    value_full = lax.all_gather(s_value, "blk", axis=0, tiled=True)
-    s_attn = student_forward(selection, info, s_query, key_full, value_full)
-
+    key_stack = jnp.concatenate([s_key] + [from_earlier(s_key, d) for d in range(1, cycle)])
+    value_stack = jnp.concatenate([s_value] + [from_earlier(s_value, d) for d in range(1, cycle)])
+    place = (my_index - selection // shard_blocks) * shard_blocks + selection % shard_blocks
+    tables = (selection, place, info)
+    s_attn = student_forward(tables, s_query, key_stack, value_stack)
+
+    grads = []
+    for s_mix, t_mix in mixed:
+        terms = project(s_attn, t_attn, s_mix, t_mix, groups)
+        grads.append(lax.psum_scatter(terms, split, scatter_dimension=0, tiled=False))
     terms = project(s_attn, t_attn, s_out, t_out, groups)
-    mismatch = lax.psum_scatter(terms, ("head", "grp"), scatter_dimension=0, tiled=False)
-    grad_attn = gradient(lax.all_gather(mismatch, ("head", "grp"), axis=0, tiled=False), s_out)
-    grad_query, grad_keys, grad_values = student_backward(
-        selection, info, s_query, grad_attn, key_full, value_full
-    )
-
-    def own(full, index):
-        return lax.dynamic_slice_in_dim(full, index * row_count, row_count, 0)
-
-    key_grads, value_grads = own(grad_keys, my_index), own(grad_values, my_index)
+    terms, grads = lax.optimization_barrier((terms, grads))
+    mismatch = lax.psum_scatter(terms, split, scatter_dimension=0, tiled=False)
+
+    grad_query, own, *far = student_backward(
+        tables, s_query, jnp.concatenate(grads, axis=1), key_stack, value_stack
+    )
     for distance in range(1, cycle):
-        owner = jnp.maximum(my_index - distance, 0)
         route = [(i, i - distance) for i in range(distance, cycle)]
-        for_keys = lax.ppermute(own(grad_keys, owner).astype(jnp.bfloat16), "blk", route)
-        for_values = lax.ppermute(own(grad_values, owner).astype(jnp.bfloat16), "blk", route)
-        key_grads = key_grads + for_keys.astype(jnp.float32)
-        value_grads = value_grads + for_values.astype(jnp.float32)
-    return (mismatch.astype(jnp.float32), grad_query, key_grads, value_grads)
+        own = own + lax.ppermute(far[distance - 1], "blk", route).astype(jnp.float32)
+    return (mismatch.astype(jnp.float32), grad_query, own[0], own[1])
 
 
 def solution(mesh):

time: 433 us -> 355 us (0.82); the launches traced: 430 us -> 357 us
  waiting for transfers between devices: 261 us -> 128 us
  matrix products: 0 us -> 24.5 us
  starting transfers between devices: 23.6 us -> 43.7 us
  local copies, waits for them, and re-layouts: 11.3 us -> 25.1 us
  blocking collectives: 12.6 us -> 0 us
  Pallas kernels: 97.8 us -> 110 us
    all_gather x3 -> x2, waiting for transfers between devices: 82 us -> 0.02 us  [on_device(): lax.all_gather(s_out[h * HD:(h + 1) * HD, :], split, axis=0, tiled=True)]
    reduce_scatter x1 -> x3, waiting for transfers between devices: 91.5 us -> 50.6 us  [the longest x2 40.8 us: on_device(): lax.psum_scatter(terms, split, scatter_dimension=0, tiled=False)]
    all_to_all x3, waiting for transfers between devices: 40.2 us -> 9.44 us  [by_head(): return lax.all_to_all(rows, 'blk', split_axis=1, concat_axis=0, tiled=True)]
    ppermute x6 -> x12, waiting for transfers between devices: 37.3 us -> 67.5 us  [the longest x3 43 us: on_device(): lax.ppermute(far[distance - 1], 'blk', route).astype(jnp.float32)]
    dot_general x0 -> x4, matrix products: none -> 24.5 us  [dot(): return lax.dot_general(a, b, dims, preferred_element_type=jnp.float32)]
    ppermute x6 -> x12, starting transfers between devices: 7.73 us -> 26.5 us  [the longest x6 16.2 us: from_earlier(): return lax.ppermute(rows, 'blk', route)]
    pallas_call x1 -> x3, Pallas kernels: 12.4 us -> 29.1 us  [project(): pl.pallas_call(project_kernel, grid=(groups,), in_specs=[pl.BlockSpec(s_a...]
    psum x1 -> x0, blocking collectives: 12.6 us -> none  [on_device(): first_count = lax.psum(jnp.sum((segments == 0).astype(jnp.int32)), 'blk')]
  transfers between devices with their start and end apart: 14 -> 21, of which waited for: 8 -> 9; matrix products, arithmetic and copies ran while one was open for 3% -> 13% of each run, Pallas kernels for 7% -> 31%
where the time goes in v2:
time: 355 us; the launch traced here: 357 us
  waiting for transfers between devices  128 us (36%)
  Pallas kernels  110 us (31%)
  starting transfers between devices  43.7 us (12%)
  local copies, waits for them, and re-layouts  25.1 us (7%)
  matrix products  24.5 us (7%)
  between operations  16.4 us (5%)
  other arithmetic  8.3 us (2%)
    ppermute x3, waiting for transfers between devices, on_device(): lax.ppermute(far[distance - 1], 'blk', route).astype(jnp.float32)  43 us
    reduce_scatter x2, waiting for transfers between devices, on_device(): lax.psum_scatter(terms, split, scatter_dimension=0, tiled=False)  40.8 us
    pallas_call x1, Pallas kernels, teacher(): pl.pallas_call(functools.partial(teacher_kernel, tile), grid_spec=pltpu.P...  34 us
    pallas_call x3, Pallas kernels, project(): pl.pallas_call(project_kernel, grid=(groups,), in_specs=[pl.BlockSpec(s_a...  29.1 us
    pallas_call x1, Pallas kernels, student_backward(): pl.pallas_call(functools.partial(backward_kernel, heads, cycle), grid_spe...  28.4 us
    dot_general x4, matrix products, dot(): return lax.dot_general(a, b, dims, preferred_element_type=jnp.float32)  24.5 us
    pallas_call x1, Pallas kernels, student_forward(): pl.pallas_call(functools.partial(forward_kernel, heads), grid_spec=pltpu....  18.7 us
    ppermute x3, waiting for transfers between devices, on_device(): first_count = first_count + lax.ppermute(count, 'blk', route)  16.3 us
  transfers between devices with their start and end apart: 21, of which 9 were waited for; matrix products, arithmetic and copies ran while one was open for 13% of the time, Pallas kernels for 31%

profile of v2, /device:TPU:0, one launch (start us, length us, event | category | flops | bytes accessed | tf_op | source)
XLA Modules:
  0.0 356.6 jit_solution(16398706723121764407)
XLA Ops:
  7.2 3.2 fusion.7
  11.2 1.2 copy_bitcast_fusion.3
  12.4 5.2 %all-to-all-start = ((bf16[1024,4,128]{2,0,1:T(8,128)(2,1)}), bf16[1024,4,128]{2,0,1:T(8,128)(2,1)S(1)}, u32[]{:S(2)}, u32[]{:S(2)}) async-start(bf16[1024,4,128]{2,0,1:T(8,128)(2,1)} %copy_bitcast_fusion.3), calls=%async_computation | async-start | bytes 2097152 | tf_op jit(solution)/shard_map/all_to_all | solution.py:308
  18.2 2.0 collective-permute-start
  20.3 1.5 collective-permute-start.1
  21.7 2.7 collective-permute-start.3
  24.4 4.0 %collective-permute-start.4 = (bf16[1024,256]{1,0:T(8,128)(2,1)}, bf16[1024,256]{1,0:T(8,128)(2,1)}, u32[]{:S(2)}, u32[]{:S(2)}) collective-permute-start(bf16[1024,256]{1,0:T(8,128)(2,1)} %param.15), channel_id=1, source_target_pairs={{0,16},{8,24},{1,17},{9,25},{2,18},{10,26},{3,19},{11,27},{4,20},{... | collective-permute-start | bytes 1572872 | tf_op jit(solution)/shard_map/ppermute | solution.py:278
  28.4 2.1 collective-permute-start.5
  30.5 1.1 copy_bitcast_fusion.2
  32.6 3.5 all-to-all-start.1
  36.1 1.2 copy_bitcast_fusion.1
  37.9 1.9 constant_dynamic-update-slice_fusion.3
  39.7 1.9 constant_dynamic-update-slice_fusion.7
  41.6 2.9 collective-permute-start.2
  45.8 1.3 collective-permute-start.6
  47.7 16.3 %collective-permute-done.2 = s32[1]{0:T(128)} collective-permute-done((s32[1]{0:T(128)}, s32[1]{0:T(128)}, u32[]{:S(2)}, u32[]{:S(2)}) %collective-permute-start.2) | collective-permute-done | bytes 36 | tf_op jit(solution)/shard_map/ppermute | solution.py:295
  64.0 1.3 collective-permute-start.7
  66.6 8.5 %all-to-all-done.1 = bf16[1024,4,128]{2,0,1:T(8,128)(2,1)S(1)} async-done(((bf16[1024,4,128]{2,0,1:T(8,128)(2,1)}), bf16[1024,4,128]{2,0,1:T(8,128)(2,1)S(1)}, u32[]{:S(2)}, u32[]{:S(2)}) %all-to-all-start.1) | async-done | bytes 1048608 | tf_op jit(solution)/shard_map/all_to_all | solution.py:308
  75.1 3.6 %all-to-all-start.2 = ((bf16[1024,4,128]{2,0,1:T(8,128)(2,1)}), bf16[1024,4,128]{2,0,1:T(8,128)(2,1)S(1)}, u32[]{:S(2)}, u32[]{:S(2)}) async-start(bf16[1024,4,128]{2,0,1:T(8,128)(2,1)} %copy_bitcast_fusion.1), calls=%async_computation.2 | async-start | bytes 2097152 | tf_op jit(solution)/shard_map/all_to_all | solution.py:308
  79.4 4.9 %collective-permute-start.8 = (bf16[1024,256]{1,0:T(8,128)(2,1)}, bf16[1024,256]{1,0:T(8,128)(2,1)S(1)}, u32[]{:S(2)}, u32[]{:S(2)}) collective-permute-start(bf16[1024,256]{1,0:T(8,128)(2,1)} %param.16), channel_id=1, source_target_pairs={{0,24},{1,25},{2,26},{3,27},{4,28},{5,29},{6,30},{7,31}} | collective-permute-start | bytes 1572872 | tf_op jit(solution)/shard_map/ppermute | solution.py:278
  84.3 1.9 constant_dynamic-update-slice_fusion.2
  86.2 1.9 constant_dynamic-update-slice_fusion.1
  88.0 1.9 constant_dynamic-update-slice_fusion.k_all
  90.8 1.2 collective-permute-done.7
  92.8 6.9 %collective-permute-done.8 = bf16[1024,256]{1,0:T(8,128)(2,1)S(1)} collective-permute-done((bf16[1024,256]{1,0:T(8,128)(2,1)}, bf16[1024,256]{1,0:T(8,128)(2,1)S(1)}, u32[]{:S(2)}, u32[]{:S(2)}) %collective-permute-start.8) | collective-permute-done | bytes 524320 | tf_op jit(solution)/shard_map/ppermute | solution.py:278
  100.5 1.0 copy-done.9
  101.5 34.0 %shard_map.130 = bf16[4096,128]{1,0:T(8,128)(2,1)} custom-call(s32[2]{0:T(128)} %pad_add_fusion.1.info_ref, bf16[4096,128]{1,0:T(8,128)(2,1)} %bitcast.50, bf16[4096,128]{1,0:T(8,128)(2,1)} %bitcast.51, bf16[4096,128]{1,0:T(8,128)(2,1)} %bitcast.52), custom_call_target="tpu_custom_call" | custom-call | flops 4294967296 | bytes 4194304 | tf_op jit(solution)/shard_map/pallas_call | solution.py:83
  135.5 4.5 %all-to-all-start.3 = ((bf16[4,1024,128]{2,1,0:T(8,128)(2,1)}), bf16[4,1024,128]{2,1,0:T(8,128)(2,1)S(1)}, u32[]{:S(2)}, u32[]{:S(2)}) async-start(bf16[4,1024,128]{2,1,0:T(8,128)(2,1)} %bitcast.53), calls=%async_computation.3 | async-start | bytes 2097152 | tf_op jit(solution)/shard_map/all_to_all | solution.py:313
  140.1 18.7 %shard_map.129.s_attn = bf16[1024,256]{1,0:T(8,128)(2,1)} custom-call(s32[16,16]{1,0:T(8,128)} %sel_ref.3, s32[16,16]{1,0:T(8,128)} %fusion.2.place_ref, s32[2]{0:T(128)} %pad_add_fusion.info_ref, bf16[1024,256]{1,0:T(8,128)(2,1)} %q_ref.3, bf16[4096,256]{1,0:T(8,128)(2,1)} %constant_dynamic-update-slice_fusion.k_all, ...), custom_call_target="tpu_custom_call" | custom-call | flops 17179869184 | bytes 4194304 | tf_op jit(solution)/shard_map/pallas_call | solution.py:206
  158.8 1.1 copy_bitcast_fusion.t_attn
  160.8 6.7 %convolution_convert_fusion.3.s_out = bf16[256,1024]{1,0:T(8,128)(2,1)} fusion(bf16[256,4096]{1,0:T(8,128)(2,1)S(1)} %copy-done.2, bf16[1024,4096]{1,0:T(8,128)(2,1)} %all-gather.3.cloned.1.call-done), kind=kOutput, calls=%fused_computation.4 | convolution fusion | flops 2147745792 | bytes 11010048 | tf_op jit(solution)/shard_map/dot_general | solution.py:22
  168.1 5.5 %convolution_convert_fusion.1.t_out = bf16[512,1024]{1,0:T(8,128)(2,1)} fusion(bf16[512,4096]{1,0:T(8,128)(2,1)S(1)} %copy-done.3, bf16[1024,4096]{1,0:T(8,128)(2,1)S(1)} %copy-done.15), kind=kOutput, calls=%fused_computation.2 | convolution fusion | flops 4295491584 | bytes 13631488 | tf_op jit(solution)/shard_map/dot_general | solution.py:22
  173.7 8.3 %shard_map.132 = bf16[8,1024,128]{2,1,0:T(8,128)(2,1)} custom-call(bf16[1024,256]{1,0:T(8,128)(2,1)} %shard_map.129.s_attn, bf16[1024,512]{1,0:T(8,128)(2,1)} %copy_bitcast_fusion.t_attn, bf16[256,1024]{1,0:T(8,128)(2,1)} %convolution_convert_fusion.3.s_out, bf16[512,1024]{1,0:T(8,128)(2,1)} %convolution_convert_fusion.1.t_out), custom_call_target="tpu_custom_call" | custom-call | tf_op jit(solution)/shard_map/pallas_call | solution.py:261
  182.3 6.7 %convolution_convert_fusion.2.s_out = bf16[256,1024]{1,0:T(8,128)(2,1)} fusion(bf16[256,4096]{1,0:T(8,128)(2,1)S(1)} %copy-done.2, bf16[1024,4096]{1,0:T(8,128)(2,1)} %all-gather.5.cloned.1.call-done), kind=kOutput, calls=%fused_computation.3 | convolution fusion | flops 2147745792 | bytes 11010048 | tf_op jit(solution)/shard_map/dot_general | solution.py:22
  189.5 5.5 %convolution_convert_fusion.t_out = bf16[512,1024]{1,0:T(8,128)(2,1)} fusion(bf16[512,4096]{1,0:T(8,128)(2,1)S(1)} %copy-done.4, bf16[1024,4096]{1,0:T(8,128)(2,1)S(1)} %copy-done.14), kind=kOutput, calls=%fused_computation.1 | convolution fusion | flops 4295491584 | bytes 13631488 | tf_op jit(solution)/shard_map/dot_general | solution.py:22
  195.0 8.4 %shard_map.133 = bf16[8,1024,128]{2,1,0:T(8,128)(2,1)} custom-call(bf16[1024,256]{1,0:T(8,128)(2,1)} %shard_map.129.s_attn, bf16[1024,512]{1,0:T(8,128)(2,1)} %copy_bitcast_fusion.t_attn, bf16[256,1024]{1,0:T(8,128)(2,1)} %convolution_convert_fusion.2.s_out, bf16[512,1024]{1,0:T(8,128)(2,1)} %convolution_convert_fusion.t_out), custom_call_target="tpu_custom_call" | custom-call | tf_op jit(solution)/shard_map/pallas_call | solution.py:261
  203.5 12.4 %shard_map.131 = bf16[8,1024,512]{2,1,0:T(8,128)(2,1)} custom-call(bf16[1024,256]{1,0:T(8,128)(2,1)} %shard_map.129.s_attn, bf16[1024,512]{1,0:T(8,128)(2,1)} %copy_bitcast_fusion.t_attn, bf16[256,4096]{1,0:T(8,128)(2,1)} %s_out.1, bf16[512,4096]{1,0:T(8,128)(2,1)} %t_out.1), custom_call_target="tpu_custom_call" | custom-call | tf_op jit(solution)/shard_map/pallas_call | solution.py:261
  215.9 4.1 %reduce-scatter.4.cloned.1.call-done = bf16[1,1024,128]{2,1,0:T(8,128)(2,1)} async-done(((bf16[8,1024,128]{2,1,0:T(8,128)(2,1)}), bf16[1,1024,128]{2,1,0:T(8,128)(2,1)}) %reduce-scatter.4.cloned.1.call-update) | async-done | bytes 262160 | tf_op jit(solution)/shard_map/reduce_scatter | solution.py:332
  220.0 36.7 %reduce-scatter.6.cloned.1.call-done = bf16[1,1024,128]{2,1,0:T(8,128)(2,1)} async-done(((bf16[8,1024,128]{2,1,0:T(8,128)(2,1)}), bf16[1,1024,128]{2,1,0:T(8,128)(2,1)}) %reduce-scatter.6.cloned.1.call-update) | async-done | bytes 262160 | tf_op jit(solution)/shard_map/reduce_scatter | solution.py:332
  258.6 28.4 %shard_map.134 = (f32[1024,256]{1,0:T(8,128)}, f32[2,1024,256]{2,1,0:T(8,128)}, bf16[2,1024,256]{2,1,0:T(8,128)(2,1)}, bf16[2,1024,256]{2,1,0:T(8,128)(2,1)}, bf16[2,1024,256]{2,1,0:T(8,128)(2,1)}) custom-call(s32[16,16]{1,0:T(8,128)} %sel_ref.3, s32[16,16]{1,0:T(8,128)} %fusion.2.place_ref, s32[2]{0:T(128)} %pad_add_fusion.info_ref, ...), custom_call_target="tpu_custom_call" | custom-call | flops 34359738368 | bytes 8388608 | tf_op jit(solution)/shard_map/pallas_call | solution.py:231
  287.0 1.3 collective-permute-start.10
  288.3 1.3 collective-permute-start.11
  289.6 1.3 collective-permute-start.9
  290.9 43.0 %collective-permute-done.10 = bf16[2,1024,256]{2,1,0:T(8,128)(2,1)S(1)} collective-permute-done((bf16[2,1024,256]{2,1,0:T(8,128)(2,1)}, bf16[2,1024,256]{2,1,0:T(8,128)(2,1)S(1)}, u32[]{:S(2)}, u32[]{:S(2)}) %collective-permute-start.10) | collective-permute-done | bytes 1048608 | tf_op jit(solution)/shard_map/ppermute | solution.py:342
  333.9 2.0 convert_add_fusion
  336.0 1.5 slice_bitcast_fusion
  337.4 9.8 %reduce-scatter.8.cloned.1.call-done = bf16[1,1024,512]{2,1,0:T(8,128)(2,1)} async-done(((bf16[8,1024,512]{2,1,0:T(8,128)(2,1)}), bf16[1,1024,512]{2,1,0:T(8,128)(2,1)}) %reduce-scatter.8.cloned.1.call-update) | async-done | bytes 1048592 | tf_op jit(solution)/shard_map/reduce_scatter | solution.py:335
  347.2 2.8 bitcast_convert_fusion
  (62 shorter events, 11.1 us)
Async XLA Ops:
  7.2 4.0 %copy-start = (bf16[1024,512]{1,0:T(8,128)(2,1)S(1)}, bf16[1024,512]{1,0:T(8,128)(2,1)}, u32[]{:S(2)}) copy-start(bf16[1024,512]{1,0:T(8,128)(2,1)} %param.10) | copy-start | bytes 3145732
  7.2 152.7 %all-gather.3.cloned.1.call-start = ((), (), s32[]{:S(2)}) async-start(), calls=%async_computation.7 | async-start | bytes 9437184 | tf_op jit(solution)/shard_map/all_gather | solution.py:301
  10.4 171.8 %all-gather.5.cloned.1.call-start = ((), (), s32[]{:S(2)}) async-start(), calls=%async_computation.9 | async-start | bytes 9437184 | tf_op jit(solution)/shard_map/all_gather | solution.py:301
  11.2 6.4 %copy-start.13 = (s32[1024]{0:T(1024)S(1)}, s32[1024]{0:T(1024)}, u32[]{:S(2)}) copy-start(s32[1024]{0:T(1024)} %param.18) | copy-start | bytes 12292
  11.2 19.3 %copy-start.5 = (bf16[1024,512]{1,0:T(8,128)(2,1)S(1)}, bf16[1024,512]{1,0:T(8,128)(2,1)}, u32[]{:S(2)}) copy-start(bf16[1024,512]{1,0:T(8,128)(2,1)} %param.11) | copy-start | bytes 3145732
  12.4 20.2 %all-to-all-start = ((bf16[1024,4,128]{2,0,1:T(8,128)(2,1)}), bf16[1024,4,128]{2,0,1:T(8,128)(2,1)S(1)}, u32[]{:S(2)}, u32[]{:S(2)}) async-start(bf16[1024,4,128]{2,0,1:T(8,128)(2,1)} %copy_bitcast_fusion.3), calls=%async_computation | async-start | bytes 2097152 | tf_op jit(solution)/shard_map/all_to_all | solution.py:308
  18.2 23.4 %collective-permute-start = (s32[1]{0:T(128)}, s32[1]{0:T(128)}, u32[]{:S(2)}, u32[]{:S(2)}) collective-permute-start(s32[1]{0:T(128)} %bitcast.1), channel_id=1, source_target_pairs={{0,8},{8,16},{16,24},{24,0},{1,9},{9,17},{17,25},{25,1},{2,10},{10... | collective-permute-start | bytes 20 | tf_op jit(solution)/shard_map/ppermute | solution.py:295
  20.3 25.5 %collective-permute-start.1 = (s32[1]{0:T(128)}, s32[1]{0:T(128)}, u32[]{:S(2)}, u32[]{:S(2)}) collective-permute-start(s32[1]{0:T(128)} %bitcast.1), channel_id=1, source_target_pairs={{0,16},{8,24},{16,0},{24,8},{1,17},{9,25},{17,1},{25,9},{2,18},{10... | collective-permute-start | bytes 20 | tf_op jit(solution)/shard_map/ppermute | solution.py:295
  21.7 57.7 %collective-permute-start.3 = (bf16[1024,256]{1,0:T(8,128)(2,1)}, bf16[1024,256]{1,0:T(8,128)(2,1)}, u32[]{:S(2)}, u32[]{:S(2)}) collective-permute-start(bf16[1024,256]{1,0:T(8,128)(2,1)} %param.15), channel_id=1, source_target_pairs={{0,8},{8,16},{16,24},{1,9},{9,17},{17,25},{2,10},{10,18},{18,26},{... | collective-permute-start | bytes 1572872 | tf_op jit(solution)/shard_map/ppermute | solution.py:278
  24.4 61.7 %collective-permute-start.4 = (bf16[1024,256]{1,0:T(8,128)(2,1)}, bf16[1024,256]{1,0:T(8,128)(2,1)}, u32[]{:S(2)}, u32[]{:S(2)}) collective-permute-start(bf16[1024,256]{1,0:T(8,128)(2,1)} %param.15), channel_id=1, source_target_pairs={{0,16},{8,24},{1,17},{9,25},{2,18},{10,26},{3,19},{11,27},{4,20},{... | collective-permute-start | bytes 1572872 | tf_op jit(solution)/shard_map/ppermute | solution.py:278
  28.4 59.6 %collective-permute-start.5 = (bf16[1024,256]{1,0:T(8,128)(2,1)}, bf16[1024,256]{1,0:T(8,128)(2,1)}, u32[]{:S(2)}, u32[]{:S(2)}) collective-permute-start(bf16[1024,256]{1,0:T(8,128)(2,1)} %param.15), channel_id=1, source_target_pairs={{0,24},{1,25},{2,26},{3,27},{4,28},{5,29},{6,30},{7,31}} | collective-permute-start | bytes 1572872 | tf_op jit(solution)/shard_map/ppermute | solution.py:278
  30.5 5.6 %copy-start.6 = (bf16[1024,512]{1,0:T(8,128)(2,1)S(1)}, bf16[1024,512]{1,0:T(8,128)(2,1)}, u32[]{:S(2)}) copy-start(bf16[1024,512]{1,0:T(8,128)(2,1)} %param.12) | copy-start | bytes 3145732
  31.6 5.6 %copy-start.12 = (s32[16,16]{1,0:T(8,128)S(1)}, s32[16,16]{1,0:T(8,128)}, u32[]{:S(2)}) copy-start(s32[16,16]{1,0:T(8,128)} %sel_ref.3) | copy-start | bytes 3076
  32.6 4.7 %copy-start.7 = (bf16[1024,4,128]{2,0,1:T(8,128)(2,1)}, bf16[1024,4,128]{2,0,1:T(8,128)(2,1)S(1)}, u32[]{:S(2)}) copy-start(bf16[1024,4,128]{2,0,1:T(8,128)(2,1)S(1)} %all-to-all-done) | copy-start | bytes 3145732
  32.6 42.6 %all-to-all-start.1 = ((bf16[1024,4,128]{2,0,1:T(8,128)(2,1)}), bf16[1024,4,128]{2,0,1:T(8,128)(2,1)S(1)}, u32[]{:S(2)}, u32[]{:S(2)}) async-start(bf16[1024,4,128]{2,0,1:T(8,128)(2,1)} %copy_bitcast_fusion.2), calls=%async_computation.1 | async-start | bytes 2097152 | tf_op jit(solution)/shard_map/all_to_all | solution.py:308
  41.6 22.4 %collective-permute-start.2 = (s32[1]{0:T(128)}, s32[1]{0:T(128)}, u32[]{:S(2)}, u32[]{:S(2)}) collective-permute-start(s32[1]{0:T(128)} %bitcast.1), channel_id=1, source_target_pairs={{0,24},{8,0},{16,8},{24,16},{1,25},{9,1},{17,9},{25,17},{2,26},{10... | collective-permute-start | bytes 20 | tf_op jit(solution)/shard_map/ppermute | solution.py:295
  45.8 44.1 %collective-permute-start.6 = (bf16[1024,256]{1,0:T(8,128)(2,1)}, bf16[1024,256]{1,0:T(8,128)(2,1)S(1)}, u32[]{:S(2)}, u32[]{:S(2)}) collective-permute-start(bf16[1024,256]{1,0:T(8,128)(2,1)} %param.16), channel_id=1, source_target_pairs={{0,8},{8,16},{16,24},{1,9},{9,17},{17,25},{2,10},{10,18},{18,26},{... | collective-permute-start | bytes 1572872 | tf_op jit(solution)/shard_map/ppermute | solution.py:278
  64.0 28.0 %collective-permute-start.7 = (bf16[1024,256]{1,0:T(8,128)(2,1)}, bf16[1024,256]{1,0:T(8,128)(2,1)S(1)}, u32[]{:S(2)}, u32[]{:S(2)}) collective-permute-start(bf16[1024,256]{1,0:T(8,128)(2,1)} %param.16), channel_id=1, source_target_pairs={{0,16},{8,24},{1,17},{9,25},{2,18},{10,26},{3,19},{11,27},{4,20},{... | collective-permute-start | bytes 1572872 | tf_op jit(solution)/shard_map/ppermute | solution.py:278
  75.1 12.9 %copy-start.8 = (bf16[1024,4,128]{2,0,1:T(8,128)(2,1)}, bf16[1024,4,128]{2,0,1:T(8,128)(2,1)S(1)}, u32[]{:S(2)}) copy-start(bf16[1024,4,128]{2,0,1:T(8,128)(2,1)S(1)} %all-to-all-done.1) | copy-start | bytes 3145732
  75.1 25.4 %all-to-all-start.2 = ((bf16[1024,4,128]{2,0,1:T(8,128)(2,1)}), bf16[1024,4,128]{2,0,1:T(8,128)(2,1)S(1)}, u32[]{:S(2)}, u32[]{:S(2)}) async-start(bf16[1024,4,128]{2,0,1:T(8,128)(2,1)} %copy_bitcast_fusion.1), calls=%async_computation.2 | async-start | bytes 2097152 | tf_op jit(solution)/shard_map/all_to_all | solution.py:308
  79.4 20.3 %collective-permute-start.8 = (bf16[1024,256]{1,0:T(8,128)(2,1)}, bf16[1024,256]{1,0:T(8,128)(2,1)S(1)}, u32[]{:S(2)}, u32[]{:S(2)}) collective-permute-start(bf16[1024,256]{1,0:T(8,128)(2,1)} %param.16), channel_id=1, source_target_pairs={{0,24},{1,25},{2,26},{3,27},{4,28},{5,29},{6,30},{7,31}} | collective-permute-start | bytes 1572872 | tf_op jit(solution)/shard_map/ppermute | solution.py:278
  100.5 1.0 copy-start.9
  135.5 23.3 %all-to-all-start.3 = ((bf16[4,1024,128]{2,1,0:T(8,128)(2,1)}), bf16[4,1024,128]{2,1,0:T(8,128)(2,1)S(1)}, u32[]{:S(2)}, u32[]{:S(2)}) async-start(bf16[4,1024,128]{2,1,0:T(8,128)(2,1)} %bitcast.53), calls=%async_computation.3 | async-start | bytes 2097152 | tf_op jit(solution)/shard_map/all_to_all | solution.py:313
  140.1 79.9 %reduce-scatter.4.cloned.1.call-start = ((), (), s32[]{:S(2)}) async-start(), calls=%async_computation.8 | async-start | bytes 2359296 | tf_op jit(solution)/shard_map/reduce_scatter | solution.py:332
  158.8 2.0 copy-start.2
  160.8 6.7 %copy-start.3 = (bf16[512,4096]{1,0:T(8,128)(2,1)S(1)}, bf16[512,4096]{1,0:T(8,128)(2,1)}, u32[]{:S(2)}) copy-start(bf16[512,4096]{1,0:T(8,128)(2,1)} %t_out.1) | copy-start | bytes 12582916
  160.8 7.4 %copy-start.15 = (bf16[1024,4096]{1,0:T(8,128)(2,1)S(1)}, bf16[1024,4096]{1,0:T(8,128)(2,1)}, u32[]{:S(2)}) copy-start(bf16[1024,4096]{1,0:T(8,128)(2,1)} %all-gather.3.cloned.1.call-done) | copy-start | bytes 25165828
  182.0 74.6 %reduce-scatter.6.cloned.1.call-start = ((), (), s32[]{:S(2)}) async-start(), calls=%async_computation.10 | async-start | bytes 2359296 | tf_op jit(solution)/shard_map/reduce_scatter | solution.py:332
  182.3 6.7 %copy-start.4 = (bf16[512,4096]{1,0:T(8,128)(2,1)S(1)}, bf16[512,4096]{1,0:T(8,128)(2,1)}, u32[]{:S(2)}) copy-start(bf16[512,4096]{1,0:T(8,128)(2,1)} %t_out.1) | copy-start | bytes 12582916
  182.3 7.2 %copy-start.14 = (bf16[1024,4096]{1,0:T(8,128)(2,1)S(1)}, bf16[1024,4096]{1,0:T(8,128)(2,1)}, u32[]{:S(2)}) copy-start(bf16[1024,4096]{1,0:T(8,128)(2,1)} %all-gather.5.cloned.1.call-done) | copy-start | bytes 25165828
  203.4 143.8 %reduce-scatter.8.cloned.1.call-start = ((), (), s32[]{:S(2)}) async-start(), calls=%async_computation.11 | async-start | bytes 9437184 | tf_op jit(solution)/shard_map/reduce_scatter | solution.py:335
  256.7 0.9 copy-start.10
  256.7 1.0 copy-start.11
  287.0 46.9 %collective-permute-start.10 = (bf16[2,1024,256]{2,1,0:T(8,128)(2,1)}, bf16[2,1024,256]{2,1,0:T(8,128)(2,1)S(1)}, u32[]{:S(2)}, u32[]{:S(2)}) collective-permute-start(bf16[2,1024,256]{2,1,0:T(8,128)(2,1)} %get-tuple-element.18), channel_id=1, source_target_pairs={{16,0},{24,8},{17,1},{25,9},{18,2},{26,10},{19,3},{27,11},{20,4},{... | collective-permute-start | bytes 3145736 | tf_op jit(solution)/shard_map/ppermute | solution.py:342
  288.3 45.6 %collective-permute-start.11 = (bf16[2,1024,256]{2,1,0:T(8,128)(2,1)}, bf16[2,1024,256]{2,1,0:T(8,128)(2,1)S(1)}, u32[]{:S(2)}, u32[]{:S(2)}) collective-permute-start(bf16[2,1024,256]{2,1,0:T(8,128)(2,1)} %get-tuple-element.19), channel_id=1, source_target_pairs={{24,0},{25,1},{26,2},{27,3},{28,4},{29,5},{30,6},{31,7}} | collective-permute-start | bytes 3145736 | tf_op jit(solution)/shard_map/ppermute | solution.py:342
  289.6 44.3 %collective-permute-start.9 = (bf16[2,1024,256]{2,1,0:T(8,128)(2,1)}, bf16[2,1024,256]{2,1,0:T(8,128)(2,1)S(1)}, u32[]{:S(2)}, u32[]{:S(2)}) collective-permute-start(bf16[2,1024,256]{2,1,0:T(8,128)(2,1)} %get-tuple-element.17), channel_id=1, source_target_pairs={{8,0},{16,8},{24,16},{9,1},{17,9},{25,17},{10,2},{18,10},{26,18},{... | collective-permute-start | bytes 3145736 | tf_op jit(solution)/shard_map/ppermute | solution.py:342
  336.0 14.1 %copy-start.1 = (bf16[1024,512]{1,0:T(8,128)(2,1)S(1)}, bf16[1024,512]{1,0:T(8,128)(2,1)}, u32[]{:S(2)}) copy-start(bf16[1024,512]{1,0:T(8,128)(2,1)} %param.10) | copy-start | bytes 3145732
Sparse Core Ops, SparseCore 0:
  10.5 84.7 all-gather.2
  96.9 80.5 all-gather.4
  182.1 37.8 reduce-scatter.3
  222.1 34.4 reduce-scatter.5
  258.8 88.3 reduce-scatter.7

commit v3 on v2

--- a/solution.py
+++ b/solution.py
@@ -74,10 +74,10 @@
     o_ref[...] = (acc / total).T.astype(jnp.bfloat16)
 
 
-def teacher(queries, keys, values, offset, first_count):
-    rows, width = queries.shape
-    tokens = keys.shape[0]
-    heads = width // HD
+def teacher(queries, keys, values, heads, columns, offset, first_count):
+    rows, tokens = queries.shape[0], keys.shape[0]
+    width = heads * HD
+    step, (q_at, k_at, v_at) = columns
     tile = 512
     info = jnp.stack([offset, first_count]).astype(jnp.int32)
     return pl.pallas_call(
@@ -86,9 +86,9 @@
             num_scalar_prefetch=1,
             grid=(heads, rows // tile),
             in_specs=[
-                pl.BlockSpec((tile, HD), lambda h, i, s: (i, h)),
-                pl.BlockSpec((tokens, HD), lambda h, i, s: (0, h)),
-                pl.BlockSpec((tokens, HD), lambda h, i, s: (0, h)),
+                pl.BlockSpec((tile, HD), lambda h, i, s: (i, step * h + q_at)),
+                pl.BlockSpec((tokens, HD), lambda h, i, s: (0, step * h + k_at)),
+                pl.BlockSpec((tokens, HD), lambda h, i, s: (0, step * h + v_at)),
             ],
             out_specs=pl.BlockSpec((tile, HD), lambda h, i, s: (i, h)),
         ),
@@ -254,7 +254,7 @@
     o_ref[0] = (dot(s_attn[...], s_out[...]) - dot(t_attn[...], t_out[...])).astype(jnp.bfloat16)
 
 
-def project(s_attn, t_attn, s_out, t_out, groups):
+def project(s_attn, t_attn, s_out, t_out, groups, s_block=0):
     rows = s_attn.shape[0]
     model = s_out.shape[1]
     tile = model // groups
@@ -264,8 +264,8 @@
         in_specs=[
             pl.BlockSpec(s_attn.shape, lambda j: (0, 0)),
             pl.BlockSpec(t_attn.shape, lambda j: (0, 0)),
-            pl.BlockSpec((s_out.shape[0], tile), lambda j: (0, j)),
-            pl.BlockSpec((t_out.shape[0], tile), lambda j: (0, j)),
+            pl.BlockSpec((s_attn.shape[1], tile), lambda j: (s_block, j)),
+            pl.BlockSpec((t_attn.shape[1], tile), lambda j: (0, j)),
         ],
         out_specs=pl.BlockSpec((1, rows, tile), lambda j: (j, 0, 0)),
         out_shape=jax.ShapeDtypeStruct((groups, rows, tile), jnp.bfloat16),
@@ -296,19 +296,24 @@
     first_count = first_count[0]
     info = jnp.stack([first_row, first_count]).astype(jnp.int32)
 
-    mixed = []
-    for h in range(s_out.shape[0] // HD):
-        part = lax.all_gather(s_out[h * HD : (h + 1) * HD, :], split, axis=0, tiled=True)
-        mixed.append(
-            (dot(s_out, part, NT).astype(jnp.bfloat16), dot(t_out, part, NT).astype(jnp.bfloat16))
-        )
+    model_cols = s_out.shape[1] // cycle
+
+    def own_cols(weights):
+        return lax.dynamic_slice_in_dim(weights, my_index * model_cols, model_cols, 1)
+
+    s_cols, t_cols = own_cols(s_out), own_cols(t_out)
+    s_cols_all = lax.all_gather(s_cols, split, axis=0, tiled=True)
+    weights = jnp.concatenate([t_cols, s_cols], axis=0)
+    mix = lax.psum(dot(weights, s_cols_all, NT).astype(jnp.bfloat16), "blk")
 
     if heads % cycle == 0:
-        def by_head(rows):
-            return lax.all_to_all(rows, "blk", split_axis=1, concat_axis=0, tiled=True)
-
+        packed = jnp.concatenate(
+            [rows.reshape(row_count, heads, HD) for rows in (t_query, t_key, t_value)], axis=2
+        ).reshape(row_count, 3 * heads * HD)
+        packed = lax.all_to_all(packed, "blk", split_axis=1, concat_axis=0, tiled=True)
+        packed, s_key, s_value = lax.optimization_barrier((packed, s_key, s_value))
         whole_heads = teacher(
-            by_head(t_query), by_head(t_key), by_head(t_value), jnp.int32(0), first_count
+            packed, packed, packed, heads // cycle, (3, (0, 1, 2)), jnp.int32(0), first_count
         )
         t_attn = lax.all_to_all(whole_heads, "blk", split_axis=0, concat_axis=1, tiled=True)
     else:
@@ -316,6 +321,8 @@
             t_query,
             lax.all_gather(t_key, "blk", axis=0, tiled=True),
             lax.all_gather(t_value, "blk", axis=0, tiled=True),
+            heads,
+            (1, (0, 0, 0)),
             first_row,
             first_count,
         )
@@ -326,16 +333,15 @@
     tables = (selection, place, info)
     s_attn = student_forward(tables, s_query, key_stack, value_stack)
 
-    grads = []
-    for s_mix, t_mix in mixed:
-        terms = project(s_attn, t_attn, s_mix, t_mix, groups)
-        grads.append(lax.psum_scatter(terms, split, scatter_dimension=0, tiled=False))
+    ratio = t_attn.shape[1] // s_attn.shape[1]
+    grad_terms = project(s_attn, t_attn, mix, mix, groups, ratio)
+    grads = lax.psum_scatter(grad_terms, split, scatter_dimension=0, tiled=False)
     terms = project(s_attn, t_attn, s_out, t_out, groups)
     terms, grads = lax.optimization_barrier((terms, grads))
     mismatch = lax.psum_scatter(terms, split, scatter_dimension=0, tiled=False)
 
     grad_query, own, *far = student_backward(
-        tables, s_query, jnp.concatenate(grads, axis=1), key_stack, value_stack
+        tables, s_query, grads, key_stack, value_stack
     )
     for distance in range(1, cycle):
         route = [(i, i - distance) for i in range(distance, cycle)]

time: 355 us -> 351 us (0.989)
  waiting for transfers between devices: 128 us -> 171 us
  matrix products: 24.5 us -> 7.42 us
  Pallas kernels: 110 us -> 93.3 us
  starting transfers between devices: 43.7 us -> 34.3 us
  local copies, waits for them, and re-layouts: 25.1 us -> 17.2 us
    psum x0 -> x1, waiting for transfers between devices: none -> 35.8 us  [on_device(): mix = lax.psum(dot(weights, s_cols_all, NT).astype(jnp.bfloat16), 'blk')]
    dot_general x4 -> x1, matrix products: 24.5 us -> 7.42 us  [dot(): return lax.dot_general(a, b, dims, preferred_element_type=jnp.float32)]
    ppermute x3, waiting for transfers between devices: 16.3 us -> 31 us  [on_device(): first_count = first_count + lax.ppermute(count, 'blk', route)]
    all_to_all x3 -> x1, waiting for transfers between devices: 9.44 us -> 0.01 us  [on_device(): lax.all_to_all(packed, 'blk', split_axis=1, concat_axis=0, tiled=True)]
    pallas_call x1, Pallas kernels: 34 us -> 24.7 us  [teacher(): pl.pallas_call(functools.partial(teacher_kernel, tile), grid_spec=pltpu.P...]
    pallas_call x3 -> x2, Pallas kernels: 29.1 us -> 21.5 us  [project(): pl.pallas_call(project_kernel, grid=(groups,), in_specs=[pl.BlockSpec(s_a...]
    all_to_all x3 -> x1, starting transfers between devices: 12.4 us -> 5.32 us  [on_device(): lax.all_to_all(packed, 'blk', split_axis=1, concat_axis=0, tiled=True)]
    ppermute x6, waiting for transfers between devices: 8.09 us -> 12.7 us  [from_earlier(): return lax.ppermute(rows, 'blk', route)]
  transfers between devices with their start and end apart: 21 -> 18, of which waited for: 9 -> 8; matrix products, arithmetic and copies ran while one was open for 13% -> 8% of each run, Pallas kernels for 31% -> 24%
where the time goes in v3:
time: 351 us; the launch traced here: 350 us
  waiting for transfers between devices  171 us (49%)
  Pallas kernels  93.3 us (27%)
  starting transfers between devices  34.3 us (10%)
  local copies, waits for them, and re-layouts  17.2 us (5%)
  between operations  16.4 us (5%)
  other arithmetic  9.57 us (3%)
  matrix products  7.42 us (2%)
    ppermute x3, waiting for transfers between devices, on_device(): lax.ppermute(far[distance - 1], 'blk', route).astype(jnp.float32)  45.9 us
    reduce_scatter x1, waiting for transfers between devices, on_device(): lax.psum_scatter(grad_terms, split, scatter_dimension=0, tiled=False)  37.6 us
    psum x1, waiting for transfers between devices, on_device(): mix = lax.psum(dot(weights, s_cols_all, NT).astype(jnp.bfloat16), 'blk')  35.8 us
    ppermute x3, waiting for transfers between devices, on_device(): first_count = first_count + lax.ppermute(count, 'blk', route)  31 us
    pallas_call x1, Pallas kernels, student_backward(): pl.pallas_call(functools.partial(backward_kernel, heads, cycle), grid_spe...  28.4 us
    pallas_call x1, Pallas kernels, teacher(): pl.pallas_call(functools.partial(teacher_kernel, tile), grid_spec=pltpu.P...  24.7 us
    pallas_call x2, Pallas kernels, project(): pl.pallas_call(project_kernel, grid=(groups,), in_specs=[pl.BlockSpec(s_a...  21.5 us
    pallas_call x1, Pallas kernels, student_forward(): pl.pallas_call(functools.partial(forward_kernel, heads), grid_spec=pltpu....  18.7 us
  transfers between devices with their start and end apart: 18, of which 8 were waited for; matrix products, arithmetic and copies ran while one was open for 8% of the time, Pallas kernels for 24%

profile of v3, /device:TPU:0, one launch (start us, length us, event | category | flops | bytes accessed | tf_op | source)
XLA Modules:
  0.0 349.7 jit_solution(7636915416026758186)
XLA Ops:
  7.3 2.0 constant_dynamic-slice_fusion
  9.5 0.4 copy_bitcast_fusion.1
  9.9 2.2 pad_maximum_fusion
  12.1 5.3 %all-to-all-start = ((bf16[1024,4,384]{2,0,1:T(8,128)(2,1)}), bf16[1024,4,384]{2,0,1:T(8,128)(2,1)}, u32[]{:S(2)}, u32[]{:S(2)}) async-start(bf16[1024,4,384]{2,0,1:T(8,128)(2,1)} %pad_maximum_fusion), calls=%async_computation | async-start | bytes 6291456 | tf_op jit(solution)/shard_map/all_to_all | solution.py:313
  17.5 0.6 convert_reduce_fusion
  18.1 3.4 collective-permute-start.2
  21.5 0.6 collective-permute-start.1
  22.0 0.5 collective-permute-start
  22.6 1.3 constant_dynamic-slice_fusion.1
  23.9 0.6 fusion.5.place_ref
  24.5 31.0 %collective-permute-done = s32[1]{0:T(128)} collective-permute-done((s32[1]{0:T(128)}, s32[1]{0:T(128)}, u32[]{:S(2)}, u32[]{:S(2)}) %collective-permute-start) | collective-permute-done | bytes 36 | tf_op jit(solution)/shard_map/ppermute | solution.py:295
  57.9 0.6 pad_add_fusion.info_ref
  58.5 0.6 pad_add_fusion.1.info_ref
  59.1 3.2 collective-permute-start.5
  62.3 2.1 collective-permute-start.4
  64.4 2.5 collective-permute-start.3
  66.9 2.1 collective-permute-start.7
  69.0 2.1 collective-permute-start.6
  71.1 7.4 %convolution_convert_fusion = bf16[768,2048]{1,0:T(8,128)(2,1)} fusion(bf16[2048,1024]{1,0:T(8,128)(2,1)} %all-gather.2.cloned.1.call-done, bf16[256,1024]{1,0:T(8,128)(2,1)S(1)} %copy-done.2, bf16[512,1024]{1,0:T(8,128)(2,1)S(1)} %constant_dynamic-slice_fusion.1), kind=kOutput, calls=%fused_computation | convolution fusion | flops 3225944064 | bytes 8912896 | tf_op jit(solution)/shard_map/dot_general | solution.py:22
  78.6 24.7 %shard_map.130 = bf16[4096,128]{1,0:T(8,128)(2,1)} custom-call(s32[2]{0:T(128)} %pad_add_fusion.1.info_ref, bf16[4096,384]{1,0:T(8,128)(2,1)} %bitcast.3.q_ref.k_ref.v_ref, bf16[4096,384]{1,0:T(8,128)(2,1)} %bitcast.3.q_ref.k_ref.v_ref, bf16[4096,384]{1,0:T(8,128)(2,1)} %bitcast.3.q_ref.k_ref.v_ref), custom_call_target="tpu_custom_call" | custom-call | flops 4294967296 | bytes 4194304 | tf_op jit(solution)/shard_map/pallas_call | solution.py:83
  103.2 0.8 constant_dynamic-update-slice_fusion.3
  104.1 0.8 constant_dynamic-update-slice_fusion.7
  104.9 3.5 %all-to-all-start.1 = ((bf16[4,1024,128]{2,1,0:T(8,128)(2,1)}), bf16[4,1024,128]{2,1,0:T(8,128)(2,1)S(1)}, u32[]{:S(2)}, u32[]{:S(2)}) async-start(bf16[4,1024,128]{2,1,0:T(8,128)(2,1)} %bitcast.4), calls=%async_computation.1 | async-start | bytes 2097152 | tf_op jit(solution)/shard_map/all_to_all | solution.py:318
  108.5 4.9 %collective-permute-start.8 = (bf16[1024,256]{1,0:T(8,128)(2,1)S(1)}, bf16[1024,256]{1,0:T(8,128)(2,1)S(1)}, u32[]{:S(2)}, u32[]{:S(2)}) collective-permute-start(bf16[1024,256]{1,0:T(8,128)(2,1)S(1)} %copy-done.6), channel_id=1, source_target_pairs={{0,24},{1,25},{2,26},{3,27},{4,28},{5,29},{6,30},{7,31}} | collective-permute-start | bytes 1572872 | tf_op jit(solution)/shard_map/ppermute | solution.py:278
  113.4 1.9 constant_dynamic-update-slice_fusion.2
  115.3 1.9 constant_dynamic-update-slice_fusion.1
  117.2 1.9 constant_dynamic-update-slice_fusion.k_all
  119.0 1.1 constant_dynamic-update-slice_fusion.6
  120.1 11.9 %collective-permute-done.7 = bf16[1024,256]{1,0:T(8,128)(2,1)} collective-permute-done((bf16[1024,256]{1,0:T(8,128)(2,1)S(1)}, bf16[1024,256]{1,0:T(8,128)(2,1)}, u32[]{:S(2)}, u32[]{:S(2)}) %collective-permute-start.7) | collective-permute-done | bytes 524320 | tf_op jit(solution)/shard_map/ppermute | solution.py:278
  132.1 1.1 constant_dynamic-update-slice_fusion.5
  133.1 0.8 collective-permute-done.8
  134.0 1.3 copy-done.8
  135.3 18.7 %shard_map.129.s_attn = bf16[1024,256]{1,0:T(8,128)(2,1)} custom-call(s32[16,16]{1,0:T(8,128)} %sel_ref.3, s32[16,16]{1,0:T(8,128)} %fusion.5.place_ref, s32[2]{0:T(128)} %pad_add_fusion.info_ref, bf16[1024,256]{1,0:T(8,128)(2,1)} %q_ref.3, bf16[4096,256]{1,0:T(8,128)(2,1)} %constant_dynamic-update-slice_fusion.k_all, bf16[4096,256]{1,0:T(8,128)(2,1)} %copy-done.8), custom_call_target="tpu_custom_call" | custom-call | flops 17179869184 | bytes 4194304 | tf_op jit(solution)/shard_map/pallas_call | solution.py:206
  154.0 1.1 copy_bitcast_fusion.t_attn
  155.1 35.8 %all-reduce.2.cloned.1.call-done.s_out.t_out = bf16[768,2048]{1,0:T(8,128)(2,1)} async-done(((bf16[768,2048]{1,0:T(8,128)(2,1)}), bf16[768,2048]{1,0:T(8,128)(2,1)}) %all-reduce.2.cloned.1.call-update) | async-done | bytes 3145744 | tf_op jit(solution)/shard_map/psum | solution.py:307
  190.9 9.1 %shard_map.132 = bf16[8,1024,256]{2,1,0:T(8,128)(2,1)} custom-call(bf16[1024,256]{1,0:T(8,128)(2,1)} %shard_map.129.s_attn, bf16[1024,512]{1,0:T(8,128)(2,1)} %copy_bitcast_fusion.t_attn, bf16[768,2048]{1,0:T(8,128)(2,1)} %all-reduce.2.cloned.1.call-done.s_out.t_out, bf16[768,2048]{1,0:T(8,128)(2,1)} %all-reduce.2.cloned.1.call-done.s_out.t_out), custom_call_target="tpu_custom_call" | custom-call | tf_op jit(solution)/shard_map/pallas_call | solution.py:261
  200.1 12.4 %shard_map.131 = bf16[8,1024,512]{2,1,0:T(8,128)(2,1)} custom-call(bf16[1024,256]{1,0:T(8,128)(2,1)} %shard_map.129.s_attn, bf16[1024,512]{1,0:T(8,128)(2,1)} %copy_bitcast_fusion.t_attn, bf16[256,4096]{1,0:T(8,128)(2,1)} %s_out.1, bf16[512,4096]{1,0:T(8,128)(2,1)} %t_out.1), custom_call_target="tpu_custom_call" | custom-call | tf_op jit(solution)/shard_map/pallas_call | solution.py:261
  212.5 37.6 %reduce-scatter.3.cloned.1.call-done = bf16[1,1024,256]{2,1,0:T(8,128)(2,1)} async-done(((bf16[8,1024,256]{2,1,0:T(8,128)(2,1)}), bf16[1,1024,256]{2,1,0:T(8,128)(2,1)}) %reduce-scatter.3.cloned.1.call-update) | async-done | bytes 524304 | tf_op jit(solution)/shard_map/reduce_scatter | solution.py:338
  250.1 28.4 %shard_map.133 = (f32[1024,256]{1,0:T(8,128)}, f32[2,1024,256]{2,1,0:T(8,128)}, bf16[2,1024,256]{2,1,0:T(8,128)(2,1)}, bf16[2,1024,256]{2,1,0:T(8,128)(2,1)}, bf16[2,1024,256]{2,1,0:T(8,128)(2,1)}) custom-call(s32[16,16]{1,0:T(8,128)} %sel_ref.3, s32[16,16]{1,0:T(8,128)} %fusion.5.place_ref, s32[2]{0:T(128)} %pad_add_fusion.info_ref, ...), custom_call_target="tpu_custom_call" | custom-call | flops 34359738368 | bytes 8388608 | tf_op jit(solution)/shard_map/pallas_call | solution.py:231
  278.5 1.3 collective-permute-start.9
  279.8 1.3 collective-permute-start.10
  281.1 1.3 collective-permute-start.11
  282.4 21.3 %collective-permute-done.9 = bf16[2,1024,256]{2,1,0:T(8,128)(2,1)S(1)} collective-permute-done((bf16[2,1024,256]{2,1,0:T(8,128)(2,1)}, bf16[2,1024,256]{2,1,0:T(8,128)(2,1)S(1)}, u32[]{:S(2)}, u32[]{:S(2)}) %collective-permute-start.9) | collective-permute-done | bytes 1048608 | tf_op jit(solution)/shard_map/ppermute | solution.py:348
  303.7 24.7 %collective-permute-done.10 = bf16[2,1024,256]{2,1,0:T(8,128)(2,1)S(1)} collective-permute-done((bf16[2,1024,256]{2,1,0:T(8,128)(2,1)}, bf16[2,1024,256]{2,1,0:T(8,128)(2,1)S(1)}, u32[]{:S(2)}, u32[]{:S(2)}) %collective-permute-start.10) | collective-permute-done | bytes 1048608 | tf_op jit(solution)/shard_map/ppermute | solution.py:348
  328.3 2.1 convert_add_fusion
  330.5 1.5 slice_bitcast_fusion
  331.9 8.3 %reduce-scatter.5.cloned.1.call-done = bf16[1,1024,512]{2,1,0:T(8,128)(2,1)} async-done(((bf16[8,1024,512]{2,1,0:T(8,128)(2,1)}), bf16[1,1024,512]{2,1,0:T(8,128)(2,1)}) %reduce-scatter.5.cloned.1.call-update) | async-done | bytes 1048592 | tf_op jit(solution)/shard_map/reduce_scatter | solution.py:341
  340.3 2.8 bitcast_convert_fusion
  (41 shorter events, 0.5 us)
Async XLA Ops:
  7.2 2.3 copy-start
  7.2 2.1 copy-start.3
  7.2 2.3 copy-start.4
  7.2 63.9 %all-gather.2.cloned.1.call-start = ((), (), s32[]{:S(2)}) async-start(), calls=%async_computation.4 | async-start | bytes 4718592 | tf_op jit(solution)/shard_map/all_gather | solution.py:305
  12.1 5.4 %copy-start.10 = (s32[1024]{0:T(1024)S(1)}, s32[1024]{0:T(1024)}, u32[]{:S(2)}) copy-start(s32[1024]{0:T(1024)} %param.18) | copy-start | bytes 12292
  12.1 47.0 %all-to-all-start = ((bf16[1024,4,384]{2,0,1:T(8,128)(2,1)}), bf16[1024,4,384]{2,0,1:T(8,128)(2,1)}, u32[]{:S(2)}, u32[]{:S(2)}) async-start(bf16[1024,4,384]{2,0,1:T(8,128)(2,1)} %pad_maximum_fusion), calls=%async_computation | async-start | bytes 6291456 | tf_op jit(solution)/shard_map/all_to_all | solution.py:313
  17.4 6.5 %copy-start.9 = (s32[16,16]{1,0:T(8,128)S(1)}, s32[16,16]{1,0:T(8,128)}, u32[]{:S(2)}) copy-start(s32[16,16]{1,0:T(8,128)} %sel_ref.3) | copy-start | bytes 3076
  17.4 41.7 %copy-start.5 = (bf16[1024,256]{1,0:T(8,128)(2,1)S(1)}, bf16[1024,256]{1,0:T(8,128)(2,1)}, u32[]{:S(2)}) copy-start(bf16[1024,256]{1,0:T(8,128)(2,1)} %param.15) | copy-start | bytes 1572868
  17.4 49.5 %copy-start.6 = (bf16[1024,256]{1,0:T(8,128)(2,1)S(1)}, bf16[1024,256]{1,0:T(8,128)(2,1)}, u32[]{:S(2)}) copy-start(bf16[1024,256]{1,0:T(8,128)(2,1)} %param.16) | copy-start | bytes 1572868
  17.4 53.7 %copy-start.2 = (bf16[256,1024]{1,0:T(8,128)(2,1)S(1)}, bf16[256,1024]{1,0:T(8,128)(2,1)}, u32[]{:S(2)}) copy-start(bf16[256,1024]{1,0:T(8,128)(2,1)} %constant_dynamic-slice_fusion) | copy-start | bytes 1572868
  17.4 173.5 %all-reduce.2.cloned.1.call-start = ((), (), s32[]{:S(2)}) async-start(), calls=%async_computation.5 | async-start | bytes 6291456 | tf_op jit(solution)/shard_map/psum | solution.py:307
  18.1 39.2 %collective-permute-start.2 = (s32[1]{0:T(128)}, s32[1]{0:T(128)}, u32[]{:S(2)}, u32[]{:S(2)}) collective-permute-start(s32[1]{0:T(128)} %bitcast.1), channel_id=1, source_target_pairs={{0,24},{8,0},{16,8},{24,16},{1,25},{9,1},{17,9},{25,17},{2,26},{10... | collective-permute-start | bytes 20 | tf_op jit(solution)/shard_map/ppermute | solution.py:295
  21.5 35.3 %collective-permute-start.1 = (s32[1]{0:T(128)}, s32[1]{0:T(128)}, u32[]{:S(2)}, u32[]{:S(2)}) collective-permute-start(s32[1]{0:T(128)} %bitcast.1), channel_id=1, source_target_pairs={{0,16},{8,24},{16,0},{24,8},{1,17},{9,25},{17,1},{25,9},{2,18},{10... | collective-permute-start | bytes 20 | tf_op jit(solution)/shard_map/ppermute | solution.py:295
  22.0 33.4 %collective-permute-start = (s32[1]{0:T(128)}, s32[1]{0:T(128)}, u32[]{:S(2)}, u32[]{:S(2)}) collective-permute-start(s32[1]{0:T(128)} %bitcast.1), channel_id=1, source_target_pairs={{0,8},{8,16},{16,24},{24,0},{1,9},{9,17},{17,25},{25,1},{2,10},{10... | collective-permute-start | bytes 20 | tf_op jit(solution)/shard_map/ppermute | solution.py:295
  59.1 58.1 %collective-permute-start.5 = (bf16[1024,256]{1,0:T(8,128)(2,1)S(1)}, bf16[1024,256]{1,0:T(8,128)(2,1)}, u32[]{:S(2)}, u32[]{:S(2)}) collective-permute-start(bf16[1024,256]{1,0:T(8,128)(2,1)S(1)} %copy-done.5), channel_id=1, source_target_pairs={{0,24},{1,25},{2,26},{3,27},{4,28},{5,29},{6,30},{7,31}} | collective-permute-start | bytes 1572872 | tf_op jit(solution)/shard_map/ppermute | solution.py:278
  62.3 53.0 %collective-permute-start.4 = (bf16[1024,256]{1,0:T(8,128)(2,1)S(1)}, bf16[1024,256]{1,0:T(8,128)(2,1)}, u32[]{:S(2)}, u32[]{:S(2)}) collective-permute-start(bf16[1024,256]{1,0:T(8,128)(2,1)S(1)} %copy-done.5), channel_id=1, source_target_pairs={{0,16},{8,24},{1,17},{9,25},{2,18},{10,26},{3,19},{11,27},{4,20},{... | collective-permute-start | bytes 1572872 | tf_op jit(solution)/shard_map/ppermute | solution.py:278
  64.4 44.1 %collective-permute-start.3 = (bf16[1024,256]{1,0:T(8,128)(2,1)S(1)}, bf16[1024,256]{1,0:T(8,128)(2,1)}, u32[]{:S(2)}, u32[]{:S(2)}) collective-permute-start(bf16[1024,256]{1,0:T(8,128)(2,1)S(1)} %copy-done.5), channel_id=1, source_target_pairs={{0,8},{8,16},{16,24},{1,9},{9,17},{17,25},{2,10},{10,18},{18,26},{... | collective-permute-start | bytes 1572872 | tf_op jit(solution)/shard_map/ppermute | solution.py:278
  66.9 65.1 %collective-permute-start.7 = (bf16[1024,256]{1,0:T(8,128)(2,1)S(1)}, bf16[1024,256]{1,0:T(8,128)(2,1)}, u32[]{:S(2)}, u32[]{:S(2)}) collective-permute-start(bf16[1024,256]{1,0:T(8,128)(2,1)S(1)} %copy-done.6), channel_id=1, source_target_pairs={{0,16},{8,24},{1,17},{9,25},{2,18},{10,26},{3,19},{11,27},{4,20},{... | collective-permute-start | bytes 1572872 | tf_op jit(solution)/shard_map/ppermute | solution.py:278
  69.0 50.0 %collective-permute-start.6 = (bf16[1024,256]{1,0:T(8,128)(2,1)S(1)}, bf16[1024,256]{1,0:T(8,128)(2,1)}, u32[]{:S(2)}, u32[]{:S(2)}) collective-permute-start(bf16[1024,256]{1,0:T(8,128)(2,1)S(1)} %copy-done.6), channel_id=1, source_target_pairs={{0,8},{8,16},{16,24},{1,9},{9,17},{17,25},{2,10},{10,18},{18,26},{... | collective-permute-start | bytes 1572872 | tf_op jit(solution)/shard_map/ppermute | solution.py:278
  104.9 49.1 %all-to-all-start.1 = ((bf16[4,1024,128]{2,1,0:T(8,128)(2,1)}), bf16[4,1024,128]{2,1,0:T(8,128)(2,1)S(1)}, u32[]{:S(2)}, u32[]{:S(2)}) async-start(bf16[4,1024,128]{2,1,0:T(8,128)(2,1)} %bitcast.4), calls=%async_computation.1 | async-start | bytes 2097152 | tf_op jit(solution)/shard_map/all_to_all | solution.py:318
  108.4 141.6 %reduce-scatter.3.cloned.1.call-start = ((), (), s32[]{:S(2)}) async-start(), calls=%async_computation.6 | async-start | bytes 4718592 | tf_op jit(solution)/shard_map/reduce_scatter | solution.py:338
  108.5 10.5 %copy-start.7 = (bf16[4096,256]{1,0:T(8,128)(2,1)S(1)}, bf16[4096,256]{1,0:T(8,128)(2,1)}, u32[]{:S(2)}) copy-start(bf16[4096,256]{1,0:T(8,128)(2,1)} %constant_dynamic-update-slice_fusion.7) | copy-start | bytes 6291460
  108.5 25.4 %collective-permute-start.8 = (bf16[1024,256]{1,0:T(8,128)(2,1)S(1)}, bf16[1024,256]{1,0:T(8,128)(2,1)S(1)}, u32[]{:S(2)}, u32[]{:S(2)}) collective-permute-start(bf16[1024,256]{1,0:T(8,128)(2,1)S(1)} %copy-done.6), channel_id=1, source_target_pairs={{0,24},{1,25},{2,26},{3,27},{4,28},{5,29},{6,30},{7,31}} | collective-permute-start | bytes 1572872 | tf_op jit(solution)/shard_map/ppermute | solution.py:278
  133.9 1.3 copy-start.8
  200.0 140.3 %reduce-scatter.5.cloned.1.call-start = ((), (), s32[]{:S(2)}) async-start(), calls=%async_computation.7 | async-start | bytes 9437184 | tf_op jit(solution)/shard_map/reduce_scatter | solution.py:341
  278.5 25.1 %collective-permute-start.9 = (bf16[2,1024,256]{2,1,0:T(8,128)(2,1)}, bf16[2,1024,256]{2,1,0:T(8,128)(2,1)S(1)}, u32[]{:S(2)}, u32[]{:S(2)}) collective-permute-start(bf16[2,1024,256]{2,1,0:T(8,128)(2,1)} %get-tuple-element.21), channel_id=1, source_target_pairs={{8,0},{16,8},{24,16},{9,1},{17,9},{25,17},{10,2},{18,10},{26,18},{... | collective-permute-start | bytes 3145736 | tf_op jit(solution)/shard_map/ppermute | solution.py:348
  279.8 48.5 %collective-permute-start.10 = (bf16[2,1024,256]{2,1,0:T(8,128)(2,1)}, bf16[2,1024,256]{2,1,0:T(8,128)(2,1)S(1)}, u32[]{:S(2)}, u32[]{:S(2)}) collective-permute-start(bf16[2,1024,256]{2,1,0:T(8,128)(2,1)} %get-tuple-element.22), channel_id=1, source_target_pairs={{16,0},{24,8},{17,1},{25,9},{18,2},{26,10},{19,3},{27,11},{20,4},{... | collective-permute-start | bytes 3145736 | tf_op jit(solution)/shard_map/ppermute | solution.py:348
  281.1 47.2 %collective-permute-start.11 = (bf16[2,1024,256]{2,1,0:T(8,128)(2,1)}, bf16[2,1024,256]{2,1,0:T(8,128)(2,1)S(1)}, u32[]{:S(2)}, u32[]{:S(2)}) collective-permute-start(bf16[2,1024,256]{2,1,0:T(8,128)(2,1)} %get-tuple-element.23), channel_id=1, source_target_pairs={{24,0},{25,1},{26,2},{27,3},{28,4},{29,5},{30,6},{31,7}} | collective-permute-start | bytes 3145736 | tf_op jit(solution)/shard_map/ppermute | solution.py:348
  330.5 12.6 %copy-start.1 = (bf16[1024,512]{1,0:T(8,128)(2,1)S(1)}, bf16[1024,512]{1,0:T(8,128)(2,1)}, u32[]{:S(2)}) copy-start(bf16[1024,512]{1,0:T(8,128)(2,1)} %param.11) | copy-start | bytes 3145732
Sparse Core Ops, SparseCore 0:
  10.2 49.5 all-gather.1
  78.7 112.1 all-reduce.1
  200.1 49.8 reduce-scatter.2
  252.2 88.0 reduce-scatter.4

commit v4 on v3

--- a/solution.py
+++ b/solution.py
@@ -254,7 +254,7 @@
     o_ref[0] = (dot(s_attn[...], s_out[...]) - dot(t_attn[...], t_out[...])).astype(jnp.bfloat16)
 
 
-def project(s_attn, t_attn, s_out, t_out, groups, s_block=0):
+def project(s_attn, t_attn, s_out, t_out, groups):
     rows = s_attn.shape[0]
     model = s_out.shape[1]
     tile = model // groups
@@ -264,13 +264,36 @@
         in_specs=[
             pl.BlockSpec(s_attn.shape, lambda j: (0, 0)),
             pl.BlockSpec(t_attn.shape, lambda j: (0, 0)),
-            pl.BlockSpec((s_attn.shape[1], tile), lambda j: (s_block, j)),
+            pl.BlockSpec((s_attn.shape[1], tile), lambda j: (0, j)),
             pl.BlockSpec((t_attn.shape[1], tile), lambda j: (0, j)),
         ],
         out_specs=pl.BlockSpec((1, rows, tile), lambda j: (j, 0, 0)),
         out_shape=jax.ShapeDtypeStruct((groups, rows, tile), jnp.bfloat16),
         compiler_params=pltpu.CompilerParams(vmem_limit_bytes=VMEM_LIMIT),
     )(s_attn, t_attn, s_out, t_out)
+
+
+def mixed_kernel(s_attn, t_attn, s_mix, t_mix, o_ref):
+    part = dot(s_attn[...], s_mix[...], NT) - dot(t_attn[...], t_mix[...], NT)
+    o_ref[0] = part.astype(jnp.bfloat16)
+
+
+def project_mixed(s_attn, t_attn, mix, groups, s_block):
+    rows = s_attn.shape[0]
+    tile = mix.shape[0] // groups
+    return pl.pallas_call(
+        mixed_kernel,
+        grid=(groups,),
+        in_specs=[
+            pl.BlockSpec(s_attn.shape, lambda j: (0, 0)),
+            pl.BlockSpec(t_attn.shape, lambda j: (0, 0)),
+            pl.BlockSpec((tile, s_attn.shape[1]), lambda j: (j, s_block)),
+            pl.BlockSpec((tile, t_attn.shape[1]), lambda j: (j, 0)),
+        ],
+        out_specs=pl.BlockSpec((1, rows, tile), lambda j: (j, 0, 0)),
+        out_shape=jax.ShapeDtypeStruct((groups, rows, tile), jnp.bfloat16),
+        compiler_params=pltpu.CompilerParams(vmem_limit_bytes=VMEM_LIMIT),
+    )(s_attn, t_attn, mix, mix)
 
 
 def from_earlier(rows, distance):
@@ -304,14 +327,14 @@
     s_cols, t_cols = own_cols(s_out), own_cols(t_out)
     s_cols_all = lax.all_gather(s_cols, split, axis=0, tiled=True)
     weights = jnp.concatenate([t_cols, s_cols], axis=0)
-    mix = lax.psum(dot(weights, s_cols_all, NT).astype(jnp.bfloat16), "blk")
-
     if heads % cycle == 0:
         packed = jnp.concatenate(
             [rows.reshape(row_count, heads, HD) for rows in (t_query, t_key, t_value)], axis=2
         ).reshape(row_count, 3 * heads * HD)
         packed = lax.all_to_all(packed, "blk", split_axis=1, concat_axis=0, tiled=True)
-        packed, s_key, s_value = lax.optimization_barrier((packed, s_key, s_value))
+        packed, s_key, s_value, s_cols_all = lax.optimization_barrier(
+            (packed, s_key, s_value, s_cols_all)
+        )
         whole_heads = teacher(
             packed, packed, packed, heads // cycle, (3, (0, 1, 2)), jnp.int32(0), first_count
         )
@@ -327,6 +350,10 @@
             first_count,
         )
 
+    mix = dot(s_cols_all, weights, NT).astype(jnp.bfloat16)
+    mix = lax.psum_scatter(mix, "blk", scatter_dimension=0, tiled=True)
+    mix = lax.all_gather(mix, "blk", axis=0, tiled=True)
+
     key_stack = jnp.concatenate([s_key] + [from_earlier(s_key, d) for d in range(1, cycle)])
     value_stack = jnp.concatenate([s_value] + [from_earlier(s_value, d) for d in range(1, cycle)])
     place = (my_index - selection // shard_blocks) * shard_blocks + selection % shard_blocks
@@ -334,7 +361,7 @@
     s_attn = student_forward(tables, s_query, key_stack, value_stack)
 
     ratio = t_attn.shape[1] // s_attn.shape[1]
-    grad_terms = project(s_attn, t_attn, mix, mix, groups, ratio)
+    grad_terms = project_mixed(s_attn, t_attn, mix, groups, ratio)
     grads = lax.psum_scatter(grad_terms, split, scatter_dimension=0, tiled=False)
     terms = project(s_attn, t_attn, s_out, t_out, groups)
     terms, grads = lax.optimization_barrier((terms, grads))

time: 351 us -> 386 us (1.100)
  waiting for transfers between devices: 171 us -> 202 us
  Pallas kernels: 93.3 us -> 102 us
    reduce_scatter x0 -> x1, waiting for transfers between devices: none -> 42.8 us  [on_device(): mix = lax.psum_scatter(mix, 'blk', scatter_dimension=0, tiled=True)]
    all_to_all x1, waiting for transfers between devices: 0.01 us -> 35.8 us  [on_device(): lax.all_to_all(packed, 'blk', split_axis=1, concat_axis=0, tiled=True)]
    psum x1 -> x0, waiting for transfers between devices: 35.8 us -> none  [on_device(): mix = lax.psum(dot(weights, s_cols_all, NT).astype(jnp.bfloat16), 'blk')]
    ppermute x3, waiting for transfers between devices: 31 us -> 3.41 us  [on_device(): first_count = first_count + lax.ppermute(count, 'blk', route)]
    pallas_call x0 -> x1, Pallas kernels: none -> 9.18 us  [project_mixed(): pl.pallas_call(mixed_kernel, grid=(groups,), in_specs=[pl.BlockSpec(s_att...]
    pallas_call x2 -> x1, Pallas kernels: 21.5 us -> 12.4 us  [project(): pl.pallas_call(project_kernel, grid=(groups,), in_specs=[pl.BlockSpec(s_a...]
    pallas_call x1, Pallas kernels: 24.7 us -> 33.7 us  [teacher(): pl.pallas_call(functools.partial(teacher_kernel, tile), grid_spec=pltpu.P...]
    ppermute x6, waiting for transfers between devices: 12.7 us -> 20.4 us  [from_earlier(): return lax.ppermute(rows, 'blk', route)]
  transfers between devices with their start and end apart: 18 -> 19, of which waited for: 8 -> 10; matrix products, arithmetic and copies ran while one was open for 8% -> 5% of each run, Pallas kernels for 24% -> 24%
where the time goes in v4:
time: 386 us; the launch traced here: 385 us
  waiting for transfers between devices  202 us (52%)
  Pallas kernels  102 us (26%)
  starting transfers between devices  31.9 us (8%)
  between operations  16.5 us (4%)
  local copies, waits for them, and re-layouts  15.2 us (4%)
  other arithmetic  9.53 us (2%)
  matrix products  7.43 us (2%)
    ppermute x3, waiting for transfers between devices, on_device(): lax.ppermute(far[distance - 1], 'blk', route).astype(jnp.float32)  45.9 us
    reduce_scatter x1, waiting for transfers between devices, on_device(): mix = lax.psum_scatter(mix, 'blk', scatter_dimension=0, tiled=True)  42.8 us
    reduce_scatter x1, waiting for transfers between devices, on_device(): lax.psum_scatter(grad_terms, split, scatter_dimension=0, tiled=False)  39.5 us
    all_to_all x1, waiting for transfers between devices, on_device(): lax.all_to_all(packed, 'blk', split_axis=1, concat_axis=0, tiled=True)  35.8 us
    pallas_call x1, Pallas kernels, teacher(): pl.pallas_call(functools.partial(teacher_kernel, tile), grid_spec=pltpu.P...  33.7 us
    pallas_call x1, Pallas kernels, student_backward(): pl.pallas_call(functools.partial(backward_kernel, heads, cycle), grid_spe...  28.4 us
    ppermute x6, waiting for transfers between devices, from_earlier(): return lax.ppermute(rows, 'blk', route)  20.4 us
    pallas_call x1, Pallas kernels, student_forward(): pl.pallas_call(functools.partial(forward_kernel, heads), grid_spec=pltpu....  18.7 us
  transfers between devices with their start and end apart: 19, of which 10 were waited for; matrix products, arithmetic and copies ran while one was open for 5% of the time, Pallas kernels for 24%

profile of v4, /device:TPU:0, one launch (start us, length us, event | category | flops | bytes accessed | tf_op | source)
XLA Modules:
  0.0 384.7 jit_solution(13209371397714637036)
XLA Ops:
  7.3 2.0 constant_dynamic-slice_fusion.1
  9.9 2.2 pad_maximum_fusion
  12.0 5.2 %all-to-all-start = ((bf16[1024,4,384]{2,0,1:T(8,128)(2,1)}), bf16[1024,4,384]{2,0,1:T(8,128)(2,1)}, u32[]{:S(2)}, u32[]{:S(2)}) async-start(bf16[1024,4,384]{2,0,1:T(8,128)(2,1)} %pad_maximum_fusion), calls=%async_computation | async-start | bytes 6291456 | tf_op jit(solution)/shard_map/all_to_all | solution.py:334
  17.2 1.4 constant_dynamic-slice_fusion
  18.6 35.8 %all-to-all-done = bf16[1024,4,384]{2,0,1:T(8,128)(2,1)} async-done(((bf16[1024,4,384]{2,0,1:T(8,128)(2,1)}), bf16[1024,4,384]{2,0,1:T(8,128)(2,1)}, u32[]{:S(2)}, u32[]{:S(2)}) %all-to-all-start) | async-done | bytes 3145760 | tf_op jit(solution)/shard_map/all_to_all | solution.py:334
  54.4 5.4 %all-gather.3.cloned.1.call-done = bf16[2048,1024]{1,0:T(8,128)(2,1)} async-done(((bf16[256,1024]{1,0:T(8,128)(2,1)}), bf16[2048,1024]{1,0:T(8,128)(2,1)}) %all-gather.3.cloned.1.call-update) | async-done | bytes 4194320 | tf_op jit(solution)/shard_map/all_gather | solution.py:328
  59.8 7.4 %convolution_convert_fusion = bf16[2048,768]{1,0:T(8,128)(2,1)} fusion(bf16[2048,1024]{1,0:T(8,128)(2,1)} %all-gather.3.cloned.1.call-done, bf16[256,1024]{1,0:T(8,128)(2,1)S(1)} %copy-done.2, bf16[512,1024]{1,0:T(8,128)(2,1)S(1)} %constant_dynamic-slice_fusion), kind=kOutput, calls=%fused_computation | convolution fusion | flops 3225944064 | bytes 8912896 | tf_op jit(solution)/shard_map/dot_general | solution.py:22
  67.3 42.8 %reduce-scatter.4.cloned.1.call-done = bf16[512,768]{1,0:T(8,128)(2,1)} async-done(((bf16[2048,768]{1,0:T(8,128)(2,1)}), bf16[512,768]{1,0:T(8,128)(2,1)}) %reduce-scatter.4.cloned.1.call-update) | async-done | bytes 786448 | tf_op jit(solution)/shard_map/reduce_scatter | solution.py:354
  110.2 0.6 convert_reduce_fusion
  110.8 1.5 collective-permute-start.2
  112.3 1.5 collective-permute-start.1
  113.8 0.5 collective-permute-start
  114.3 0.6 fusion.5.place_ref
  114.9 3.4 collective-permute-done
  120.9 0.6 pad_add_fusion.info_ref
  121.5 0.6 pad_add_fusion.1.info_ref
  122.0 1.7 collective-permute-start.5
  123.8 2.2 collective-permute-start.4
  126.0 3.2 collective-permute-start.3
  129.2 1.3 collective-permute-start.7
  130.5 2.1 collective-permute-start.6
  132.6 33.7 %shard_map.130 = bf16[4096,128]{1,0:T(8,128)(2,1)} custom-call(s32[2]{0:T(128)} %pad_add_fusion.1.info_ref, bf16[4096,384]{1,0:T(8,128)(2,1)} %bitcast.3.q_ref.k_ref.v_ref, bf16[4096,384]{1,0:T(8,128)(2,1)} %bitcast.3.q_ref.k_ref.v_ref, bf16[4096,384]{1,0:T(8,128)(2,1)} %bitcast.3.q_ref.k_ref.v_ref), custom_call_target="tpu_custom_call" | custom-call | flops 4294967296 | bytes 4194304 | tf_op jit(solution)/shard_map/pallas_call | solution.py:83
  166.4 0.8 constant_dynamic-update-slice_fusion.3
  167.2 0.8 constant_dynamic-update-slice_fusion.7
  168.0 3.5 all-to-all-start.1
  171.6 4.9 %collective-permute-start.8 = (bf16[1024,256]{1,0:T(8,128)(2,1)S(1)}, bf16[1024,256]{1,0:T(8,128)(2,1)S(1)}, u32[]{:S(2)}, u32[]{:S(2)}) collective-permute-start(bf16[1024,256]{1,0:T(8,128)(2,1)S(1)} %copy-done.6), channel_id=1, source_target_pairs={{0,24},{1,25},{2,26},{3,27},{4,28},{5,29},{6,30},{7,31}} | collective-permute-start | bytes 1572872 | tf_op jit(solution)/shard_map/ppermute | solution.py:301
  176.5 1.9 constant_dynamic-update-slice_fusion.2
  178.4 1.9 constant_dynamic-update-slice_fusion.1
  180.3 0.8 constant_dynamic-update-slice_fusion.k_all
  181.1 1.1 constant_dynamic-update-slice_fusion.6
  182.2 9.8 %collective-permute-done.7 = bf16[1024,256]{1,0:T(8,128)(2,1)S(1)} collective-permute-done((bf16[1024,256]{1,0:T(8,128)(2,1)S(1)}, bf16[1024,256]{1,0:T(8,128)(2,1)S(1)}, u32[]{:S(2)}, u32[]{:S(2)}) %collective-permute-start.7) | collective-permute-done | bytes 524320 | tf_op jit(solution)/shard_map/ppermute | solution.py:301
  192.1 10.6 %collective-permute-done.8 = bf16[1024,256]{1,0:T(8,128)(2,1)S(1)} collective-permute-done((bf16[1024,256]{1,0:T(8,128)(2,1)S(1)}, bf16[1024,256]{1,0:T(8,128)(2,1)S(1)}, u32[]{:S(2)}, u32[]{:S(2)}) %collective-permute-start.8) | collective-permute-done | bytes 524320 | tf_op jit(solution)/shard_map/ppermute | solution.py:301
  202.7 1.3 copy-done.8
  204.0 18.7 %shard_map.129.s_attn = bf16[1024,256]{1,0:T(8,128)(2,1)} custom-call(s32[16,16]{1,0:T(8,128)} %sel_ref.3, s32[16,16]{1,0:T(8,128)} %fusion.5.place_ref, s32[2]{0:T(128)} %pad_add_fusion.info_ref, bf16[1024,256]{1,0:T(8,128)(2,1)} %q_ref.3, bf16[4096,256]{1,0:T(8,128)(2,1)} %constant_dynamic-update-slice_fusion.k_all, bf16[4096,256]{1,0:T(8,128)(2,1)} %copy-done.8), custom_call_target="tpu_custom_call" | custom-call | flops 17179869184 | bytes 4194304 | tf_op jit(solution)/shard_map/pallas_call | solution.py:206
  222.7 1.1 copy_bitcast_fusion.t_attn
  223.8 9.2 %shard_map.132 = bf16[8,1024,256]{2,1,0:T(8,128)(2,1)} custom-call(bf16[1024,256]{1,0:T(8,128)(2,1)} %shard_map.129.s_attn, bf16[1024,512]{1,0:T(8,128)(2,1)} %copy_bitcast_fusion.t_attn, bf16[2048,768]{1,0:T(8,128)(2,1)} %all-gather.5.cloned.1.call-done.s_mix.t_mix, bf16[2048,768]{1,0:T(8,128)(2,1)} %all-gather.5.cloned.1.call-done.s_mix.t_mix), custom_call_target="tpu_custom_call" | custom-call | tf_op jit(solution)/shard_map/pallas_call | solution.py:284
  233.2 12.4 %shard_map.131 = bf16[8,1024,512]{2,1,0:T(8,128)(2,1)} custom-call(bf16[1024,256]{1,0:T(8,128)(2,1)} %shard_map.129.s_attn, bf16[1024,512]{1,0:T(8,128)(2,1)} %copy_bitcast_fusion.t_attn, bf16[256,4096]{1,0:T(8,128)(2,1)} %s_out.1, bf16[512,4096]{1,0:T(8,128)(2,1)} %t_out.1), custom_call_target="tpu_custom_call" | custom-call | tf_op jit(solution)/shard_map/pallas_call | solution.py:261
  245.6 39.5 %reduce-scatter.6.cloned.1.call-done = bf16[1,1024,256]{2,1,0:T(8,128)(2,1)} async-done(((bf16[8,1024,256]{2,1,0:T(8,128)(2,1)}), bf16[1,1024,256]{2,1,0:T(8,128)(2,1)}) %reduce-scatter.6.cloned.1.call-update) | async-done | bytes 524304 | tf_op jit(solution)/shard_map/reduce_scatter | solution.py:365
  285.2 28.4 %shard_map.133 = (f32[1024,256]{1,0:T(8,128)}, f32[2,1024,256]{2,1,0:T(8,128)}, bf16[2,1024,256]{2,1,0:T(8,128)(2,1)}, bf16[2,1024,256]{2,1,0:T(8,128)(2,1)}, bf16[2,1024,256]{2,1,0:T(8,128)(2,1)}) custom-call(s32[16,16]{1,0:T(8,128)} %sel_ref.3, s32[16,16]{1,0:T(8,128)} %fusion.5.place_ref, s32[2]{0:T(128)} %pad_add_fusion.info_ref, ...), custom_call_target="tpu_custom_call" | custom-call | flops 34359738368 | bytes 8388608 | tf_op jit(solution)/shard_map/pallas_call | solution.py:231
  313.6 1.3 collective-permute-start.9
  314.9 1.3 collective-permute-start.10
  316.2 1.3 collective-permute-start.11
  317.5 21.2 %collective-permute-done.9 = bf16[2,1024,256]{2,1,0:T(8,128)(2,1)S(1)} collective-permute-done((bf16[2,1024,256]{2,1,0:T(8,128)(2,1)}, bf16[2,1024,256]{2,1,0:T(8,128)(2,1)S(1)}, u32[]{:S(2)}, u32[]{:S(2)}) %collective-permute-start.9) | collective-permute-done | bytes 1048608 | tf_op jit(solution)/shard_map/ppermute | solution.py:375
  338.7 24.7 %collective-permute-done.10 = bf16[2,1024,256]{2,1,0:T(8,128)(2,1)S(1)} collective-permute-done((bf16[2,1024,256]{2,1,0:T(8,128)(2,1)}, bf16[2,1024,256]{2,1,0:T(8,128)(2,1)S(1)}, u32[]{:S(2)}, u32[]{:S(2)}) %collective-permute-start.10) | collective-permute-done | bytes 1048608 | tf_op jit(solution)/shard_map/ppermute | solution.py:375
  363.4 2.1 convert_add_fusion
  365.6 1.5 slice_bitcast_fusion
  367.0 8.3 %reduce-scatter.8.cloned.1.call-done = bf16[1,1024,512]{2,1,0:T(8,128)(2,1)} async-done(((bf16[8,1024,512]{2,1,0:T(8,128)(2,1)}), bf16[1,1024,512]{2,1,0:T(8,128)(2,1)}) %reduce-scatter.8.cloned.1.call-update) | async-done | bytes 1048592 | tf_op jit(solution)/shard_map/reduce_scatter | solution.py:368
  375.3 2.8 bitcast_convert_fusion
  (44 shorter events, 1.1 us)
Async XLA Ops:
  7.2 2.3 copy-start
  7.2 2.1 copy-start.3
  7.2 2.3 copy-start.4
  7.2 52.6 %all-gather.3.cloned.1.call-start = ((), (), s32[]{:S(2)}) async-start(), calls=%async_computation.5 | async-start | bytes 4718592 | tf_op jit(solution)/shard_map/all_gather | solution.py:328
  12.0 42.4 %all-to-all-start = ((bf16[1024,4,384]{2,0,1:T(8,128)(2,1)}), bf16[1024,4,384]{2,0,1:T(8,128)(2,1)}, u32[]{:S(2)}, u32[]{:S(2)}) async-start(bf16[1024,4,384]{2,0,1:T(8,128)(2,1)} %pad_maximum_fusion), calls=%async_computation | async-start | bytes 6291456 | tf_op jit(solution)/shard_map/all_to_all | solution.py:334
  17.2 42.6 %copy-start.2 = (bf16[256,1024]{1,0:T(8,128)(2,1)S(1)}, bf16[256,1024]{1,0:T(8,128)(2,1)}, u32[]{:S(2)}) copy-start(bf16[256,1024]{1,0:T(8,128)(2,1)} %constant_dynamic-slice_fusion.1) | copy-start | bytes 1572868
  17.2 92.9 %reduce-scatter.4.cloned.1.call-start = ((), (), s32[]{:S(2)}) async-start(), calls=%async_computation.6 | async-start | bytes 3932160 | tf_op jit(solution)/shard_map/reduce_scatter | solution.py:354
  67.2 42.9 %copy-start.10 = (s32[1024]{0:T(1024)S(1)}, s32[1024]{0:T(1024)}, u32[]{:S(2)}) copy-start(s32[1024]{0:T(1024)} %param.18) | copy-start | bytes 12292
  67.2 47.1 %copy-start.9 = (s32[16,16]{1,0:T(8,128)S(1)}, s32[16,16]{1,0:T(8,128)}, u32[]{:S(2)}) copy-start(s32[16,16]{1,0:T(8,128)} %sel_ref.3) | copy-start | bytes 3076
  67.2 54.8 %copy-start.5 = (bf16[1024,256]{1,0:T(8,128)(2,1)S(1)}, bf16[1024,256]{1,0:T(8,128)(2,1)}, u32[]{:S(2)}) copy-start(bf16[1024,256]{1,0:T(8,128)(2,1)} %param.15) | copy-start | bytes 1572868
  67.2 61.9 %copy-start.6 = (bf16[1024,256]{1,0:T(8,128)(2,1)S(1)}, bf16[1024,256]{1,0:T(8,128)(2,1)}, u32[]{:S(2)}) copy-start(bf16[1024,256]{1,0:T(8,128)(2,1)} %param.16) | copy-start | bytes 1572868
  67.3 156.5 %all-gather.5.cloned.1.call-start = ((), (), s32[]{:S(2)}) async-start(), calls=%async_computation.7 | async-start | bytes 3932160 | tf_op jit(solution)/shard_map/all_gather | solution.py:355
  110.8 9.4 %collective-permute-start.2 = (s32[1]{0:T(128)}, s32[1]{0:T(128)}, u32[]{:S(2)}, u32[]{:S(2)}) collective-permute-start(s32[1]{0:T(128)} %bitcast.1), channel_id=1, source_target_pairs={{0,24},{8,0},{16,8},{24,16},{1,25},{9,1},{17,9},{25,17},{2,26},{10... | collective-permute-start | bytes 20 | tf_op jit(solution)/shard_map/ppermute | solution.py:318
  112.3 7.3 %collective-permute-start.1 = (s32[1]{0:T(128)}, s32[1]{0:T(128)}, u32[]{:S(2)}, u32[]{:S(2)}) collective-permute-start(s32[1]{0:T(128)} %bitcast.1), channel_id=1, source_target_pairs={{0,16},{8,24},{16,0},{24,8},{1,17},{9,25},{17,1},{25,9},{2,18},{10... | collective-permute-start | bytes 20 | tf_op jit(solution)/shard_map/ppermute | solution.py:318
  113.8 4.6 %collective-permute-start = (s32[1]{0:T(128)}, s32[1]{0:T(128)}, u32[]{:S(2)}, u32[]{:S(2)}) collective-permute-start(s32[1]{0:T(128)} %bitcast.1), channel_id=1, source_target_pairs={{0,8},{8,16},{16,24},{24,0},{1,9},{9,17},{17,25},{25,1},{2,10},{10... | collective-permute-start | bytes 20 | tf_op jit(solution)/shard_map/ppermute | solution.py:318
  122.0 58.2 %collective-permute-start.5 = (bf16[1024,256]{1,0:T(8,128)(2,1)S(1)}, bf16[1024,256]{1,0:T(8,128)(2,1)S(1)}, u32[]{:S(2)}, u32[]{:S(2)}) collective-permute-start(bf16[1024,256]{1,0:T(8,128)(2,1)S(1)} %copy-done.5), channel_id=1, source_target_pairs={{0,24},{1,25},{2,26},{3,27},{4,28},{5,29},{6,30},{7,31}} | collective-permute-start | bytes 1572872 | tf_op jit(solution)/shard_map/ppermute | solution.py:301
  123.8 54.6 %collective-permute-start.4 = (bf16[1024,256]{1,0:T(8,128)(2,1)S(1)}, bf16[1024,256]{1,0:T(8,128)(2,1)}, u32[]{:S(2)}, u32[]{:S(2)}) collective-permute-start(bf16[1024,256]{1,0:T(8,128)(2,1)S(1)} %copy-done.5), channel_id=1, source_target_pairs={{0,16},{8,24},{1,17},{9,25},{2,18},{10,26},{3,19},{11,27},{4,20},{... | collective-permute-start | bytes 1572872 | tf_op jit(solution)/shard_map/ppermute | solution.py:301
  126.0 45.6 %collective-permute-start.3 = (bf16[1024,256]{1,0:T(8,128)(2,1)S(1)}, bf16[1024,256]{1,0:T(8,128)(2,1)}, u32[]{:S(2)}, u32[]{:S(2)}) collective-permute-start(bf16[1024,256]{1,0:T(8,128)(2,1)S(1)} %copy-done.5), channel_id=1, source_target_pairs={{0,8},{8,16},{16,24},{1,9},{9,17},{17,25},{2,10},{10,18},{18,26},{... | collective-permute-start | bytes 1572872 | tf_op jit(solution)/shard_map/ppermute | solution.py:301
  129.2 62.9 %collective-permute-start.7 = (bf16[1024,256]{1,0:T(8,128)(2,1)S(1)}, bf16[1024,256]{1,0:T(8,128)(2,1)S(1)}, u32[]{:S(2)}, u32[]{:S(2)}) collective-permute-start(bf16[1024,256]{1,0:T(8,128)(2,1)S(1)} %copy-done.6), channel_id=1, source_target_pairs={{0,16},{8,24},{1,17},{9,25},{2,18},{10,26},{3,19},{11,27},{4,20},{... | collective-permute-start | bytes 1572872 | tf_op jit(solution)/shard_map/ppermute | solution.py:301
  130.5 50.6 %collective-permute-start.6 = (bf16[1024,256]{1,0:T(8,128)(2,1)S(1)}, bf16[1024,256]{1,0:T(8,128)(2,1)}, u32[]{:S(2)}, u32[]{:S(2)}) collective-permute-start(bf16[1024,256]{1,0:T(8,128)(2,1)S(1)} %copy-done.6), channel_id=1, source_target_pairs={{0,8},{8,16},{16,24},{1,9},{9,17},{17,25},{2,10},{10,18},{18,26},{... | collective-permute-start | bytes 1572872 | tf_op jit(solution)/shard_map/ppermute | solution.py:301
  168.0 54.7 %all-to-all-start.1 = ((bf16[4,1024,128]{2,1,0:T(8,128)(2,1)}), bf16[4,1024,128]{2,1,0:T(8,128)(2,1)S(1)}, u32[]{:S(2)}, u32[]{:S(2)}) async-start(bf16[4,1024,128]{2,1,0:T(8,128)(2,1)} %bitcast.4), calls=%async_computation.1 | async-start | bytes 2097152 | tf_op jit(solution)/shard_map/all_to_all | solution.py:341
  171.6 113.6 %reduce-scatter.6.cloned.1.call-start = ((), (), s32[]{:S(2)}) async-start(), calls=%async_computation.8 | async-start | bytes 4718592 | tf_op jit(solution)/shard_map/reduce_scatter | solution.py:365
  171.6 9.5 %copy-start.7 = (bf16[4096,256]{1,0:T(8,128)(2,1)S(1)}, bf16[4096,256]{1,0:T(8,128)(2,1)}, u32[]{:S(2)}) copy-start(bf16[4096,256]{1,0:T(8,128)(2,1)} %constant_dynamic-update-slice_fusion.7) | copy-start | bytes 6291460
  171.6 31.0 %collective-permute-start.8 = (bf16[1024,256]{1,0:T(8,128)(2,1)S(1)}, bf16[1024,256]{1,0:T(8,128)(2,1)S(1)}, u32[]{:S(2)}, u32[]{:S(2)}) collective-permute-start(bf16[1024,256]{1,0:T(8,128)(2,1)S(1)} %copy-done.6), channel_id=1, source_target_pairs={{0,24},{1,25},{2,26},{3,27},{4,28},{5,29},{6,30},{7,31}} | collective-permute-start | bytes 1572872 | tf_op jit(solution)/shard_map/ppermute | solution.py:301
  202.7 1.3 copy-start.8
  233.0 142.3 %reduce-scatter.8.cloned.1.call-start = ((), (), s32[]{:S(2)}) async-start(), calls=%async_computation.9 | async-start | bytes 9437184 | tf_op jit(solution)/shard_map/reduce_scatter | solution.py:368
  313.6 25.1 %collective-permute-start.9 = (bf16[2,1024,256]{2,1,0:T(8,128)(2,1)}, bf16[2,1024,256]{2,1,0:T(8,128)(2,1)S(1)}, u32[]{:S(2)}, u32[]{:S(2)}) collective-permute-start(bf16[2,1024,256]{2,1,0:T(8,128)(2,1)} %get-tuple-element.23), channel_id=1, source_target_pairs={{8,0},{16,8},{24,16},{9,1},{17,9},{25,17},{10,2},{18,10},{26,18},{... | collective-permute-start | bytes 3145736 | tf_op jit(solution)/shard_map/ppermute | solution.py:375
  314.9 48.5 %collective-permute-start.10 = (bf16[2,1024,256]{2,1,0:T(8,128)(2,1)}, bf16[2,1024,256]{2,1,0:T(8,128)(2,1)S(1)}, u32[]{:S(2)}, u32[]{:S(2)}) collective-permute-start(bf16[2,1024,256]{2,1,0:T(8,128)(2,1)} %get-tuple-element.24), channel_id=1, source_target_pairs={{16,0},{24,8},{17,1},{25,9},{18,2},{26,10},{19,3},{27,11},{20,4},{... | collective-permute-start | bytes 3145736 | tf_op jit(solution)/shard_map/ppermute | solution.py:375
  316.2 47.2 %collective-permute-start.11 = (bf16[2,1024,256]{2,1,0:T(8,128)(2,1)}, bf16[2,1024,256]{2,1,0:T(8,128)(2,1)S(1)}, u32[]{:S(2)}, u32[]{:S(2)}) collective-permute-start(bf16[2,1024,256]{2,1,0:T(8,128)(2,1)} %get-tuple-element.25), channel_id=1, source_target_pairs={{24,0},{25,1},{26,2},{27,3},{28,4},{29,5},{30,6},{31,7}} | collective-permute-start | bytes 3145736 | tf_op jit(solution)/shard_map/ppermute | solution.py:375
  365.6 12.6 %copy-start.1 = (bf16[1024,512]{1,0:T(8,128)(2,1)S(1)}, bf16[1024,512]{1,0:T(8,128)(2,1)}, u32[]{:S(2)}) copy-start(bf16[1024,512]{1,0:T(8,128)(2,1)} %param.11) | copy-start | bytes 3145732
Sparse Core Ops, SparseCore 0:
  10.2 49.5 all-gather.2
  67.4 42.6 reduce-scatter.3
  112.0 89.9 all-gather.4
  233.1 51.9 reduce-scatter.5
  287.3 87.9 reduce-scatter.7
